TPU v7x, 128 devices: a whole 4x4x4 slice. The times are simulated.
128 devices in a mesh: prow: 16 (over z, y_lo, core), pcol: 8 (over x, y_hi).
Axes of the slice: x: 4, y: 4 (y_hi: 2, y_lo: 2; y = y_hi * 2 + y_lo), z: 4, core: 2. Of those that a mesh axis runs over, the one named last changes fastest.
Arguments:
- grace_slab: float32 [90112, 2048], P('prow', 'pcol'), may hold values from -6 to 6
- goce_slab: float32 [90112, 2048], P('prow', 'pcol'), may hold values from -6 to 240
- grace_weight: float32 [1], replicated, may hold values from 0.8 to 1.25
- goce_weight: float32 [1], replicated, may hold values from 0.8 to 1.25
- kaula_prior: float32 [2048], P('pcol'), may hold values from 2 to 20
- row_target: int32 [90112], replicated, may hold values from 0 to 90111, as said below
- column_target: int32 [2048], replicated, may hold values from 0 to 2047, as said below
Outputs:
- factored: float32 [90112, 2048], P('prow', 'pcol')
Inputs may be any that keep to these rules, and one draw needn't show every extreme that they name: `row_target`: a permutation; each aligned block of 5632 entries holds exactly 352 values in each aligned range of 5632 values. `column_target`: a permutation; each aligned block of 256 entries holds exactly 32 values in each aligned range of 256 values.
All inputs are finite; a program needn't handle non-finite values.
Results may differ from a plain program's by a relative error of at most 0.00005.
Values sent between devices are 32-bit elements; how exact they have to be, the bound alone decides.
A program may use at most 128 MiB of HBM per device.

v0:
```python
import jax
import jax.numpy as jnp
from jax import lax
from jax.sharding import PartitionSpec as P

SLAB = 2048
PANEL = 512
BLOCK = 128


def order_index(amount, device, groups, block_size):
    local = jnp.arange(amount, dtype=jnp.int32)
    return (local // block_size * groups + device) * block_size + local % block_size


def to_order(gathered, row_devices, per_device):
    width = gathered.shape[1]
    shaped = gathered.reshape(row_devices, per_device, BLOCK, width)
    return shaped.transpose(1, 0, 2, 3).reshape(-1, width)


def factor_rows(raw_rows, order_rows, factor, inverse):
    solved = jnp.dot(raw_rows, inverse.T, precision=lax.Precision.HIGHEST)
    known = jnp.take(factor, jnp.minimum(order_rows, PANEL - 1), axis=0)
    return jnp.where(order_rows[:, None] < PANEL, known, solved)


def cholesky_block(diag_block):
    symmetric = jnp.tril(diag_block) + jnp.tril(diag_block, -1).T
    factor = jnp.linalg.cholesky(symmetric)
    inverse = jax.scipy.linalg.solve_triangular(
        factor, jnp.eye(PANEL, dtype=jnp.float32), lower=True
    )
    return (factor, inverse)


def placement(targets, owners, device, amount):
    sources = lax.dynamic_slice_in_dim(jnp.argsort(owners, stable=True), device * amount, amount)
    places = jnp.take(targets, sources) - device * amount
    return jnp.argsort(places)


def shards(
    grace_slab, goce_slab, grace_weight, goce_weight, kaula_prior, row_target, column_target
):
    row_devices = lax.axis_size("prow")
    col_devices = lax.axis_size("pcol")
    row_id = lax.axis_index("prow")
    col_id = lax.axis_index("pcol")
    rows_here, cols_here = grace_slab.shape
    row_owner = row_target // rows_here
    col_owner = column_target // cols_here
    send_rows = jnp.argsort(
        lax.dynamic_slice_in_dim(row_owner, row_id * rows_here, rows_here), stable=True
    )
    send_cols = jnp.argsort(
        lax.dynamic_slice_in_dim(col_owner, col_id * cols_here, cols_here), stable=True
    )
    outgoing = jnp.take(jnp.take(grace_slab, send_rows, axis=0), send_cols, axis=1)
    row_group = rows_here // row_devices
    packed = (
        outgoing.reshape(row_devices, row_group, cols_here)
        .transpose(1, 0, 2)
        .reshape(row_group, row_devices * cols_here)
    )
    received = lax.all_to_all(packed, ("prow", "pcol"), split_axis=1, concat_axis=1, tiled=True)
    arrived = (
        received.reshape(row_group, row_devices, cols_here)
        .transpose(1, 0, 2)
        .reshape(rows_here, cols_here)
    )
    arrived = jnp.take(arrived, placement(row_target, row_owner, row_id, rows_here), axis=0)
    arrived = jnp.take(arrived, placement(column_target, col_owner, col_id, cols_here), axis=1)
    order_rows = order_index(rows_here, row_id, row_devices, BLOCK)
    order_cols = order_index(cols_here, col_id, col_devices, BLOCK)
    on_diagonal = order_rows[:, None] == order_cols[None, :]
    combined = grace_weight[0] * arrived + goce_weight[0] * goce_slab
    combined = combined + jnp.where(on_diagonal, kaula_prior[None, :], 0.0)
    first_block = combined[:, :BLOCK]
    panel_block = lax.all_gather(first_block, "pcol", axis=1, tiled=True)[:, :PANEL]
    per_device = SLAB // (BLOCK * row_devices)
    raw_rows = to_order(
        lax.all_gather(panel_block[:BLOCK], "prow", axis=0, tiled=True), row_devices, 1
    )
    factor, inverse = cholesky_block(raw_rows[:PANEL])
    local_factors = factor_rows(panel_block, order_rows, factor, inverse)
    leading = to_order(
        lax.all_gather(local_factors[: per_device * BLOCK], "prow", axis=0, tiled=True),
        row_devices,
        per_device,
    )
    col_factors = jnp.take(leading, order_cols, axis=0)
    update = combined - jnp.dot(local_factors, col_factors.T, precision=lax.Precision.HIGHEST)
    panel_part = jnp.take(local_factors, jnp.minimum(order_cols, PANEL - 1), axis=1)
    kept = jnp.where(order_rows[:, None] < PANEL, combined, update)
    return jnp.where(order_cols[None, :] < PANEL, panel_part, kept)


def solution(mesh):
    return jax.shard_map(
        shards,
        mesh=mesh,
        in_specs=(P("prow", "pcol"), P("prow", "pcol"), P(), P(), P("pcol"), P(), P()),
        out_specs=P("prow", "pcol"),
        check_vma=False,
    )
```

profile of v0, /device:TPU:7, one launch (start us, length us, event | category | flops | bytes accessed | tf_op | source)
XLA Modules:
  0.0 845.7 jit_solution(318927713755525837)
XLA Ops:
  29.0 16.9 %gather_fusion.5 = f32[5632,256]{1,0:T(8,128)} fusion(f32[5632,256]{1,0:T(8,128)} %param.11, s32[6144]{0:T(1024)S(1)} %pad_clamp_fusion.2), kind=kCustom, calls=%fused_computation.clone | custom fusion | bytes 11556864 | tf_op jit(solution)/shard_map/jit(_take)/gather | solution.py:59
  45.9 7.6 broadcast_select_fusion.1
  59.7 9.9 %gather_fusion.6 = f32[256,5632]{1,0:T(8,128)} fusion(f32[5632,256]{0,1:T(8,128)} %copy.15, s32[1024]{0:T(1024)S(1)} %pad_clamp_fusion.7), kind=kCustom, calls=%fused_computation.1.clone | custom fusion | bytes 11535360 | tf_op jit(solution)/shard_map/jit(_take)/gather | solution.py:59
  88.1 11.2 %all-to-all-start = ((f32[352,128,32]{0,2,1:T(8,128)}), f32[352,128,32]{0,2,1:T(8,128)}, u32[]{:S(2)}, u32[]{:S(2)}) async-start(f32[352,128,32]{0,2,1:T(8,128)} %bitcast.76), calls=%async_computation | async-start | bytes 12582912 | tf_op jit(solution)/shard_map/all_to_all | solution.py:66
  99.4 71.5 %sort.104 = (s32[90112]{0:T(1024)}, s32[90112]{0:T(1024)S(1)}) sort(s32[90112]{0:T(1024)S(1)} %add_select_fusion, s32[90112]{0:T(1024)S(1)} %iota.185), dimensions={0}, to_apply=%region_2.5 | sort | flops 1531904 | bytes 1441792 | tf_op jit(solution)/shard_map/jit(argsort)/sort | solution.py:38
  171.0 29.3 %gather_fusion = s32[5632]{0:T(1024)S(1)} fusion(s32[90112]{0:T(1024)S(1)} %copy-done, s32[6144]{0:T(1024)S(1)} %pad_clamp_fusion.3), kind=kCustom, calls=%fused_computation.4 | custom fusion | bytes 67584 | tf_op jit(solution)/shard_map/jit(_take)/gather | solution.py:39
  214.9 16.8 %gather_fusion.7 = f32[5632,256]{1,0:T(8,128)} fusion(f32[5632,256]{1,0:T(8,128)} %bitcast.75, s32[6144]{0:T(1024)S(1)} %pad_clamp_fusion.1), kind=kCustom, calls=%fused_computation.2.clone | custom fusion | bytes 11556864 | tf_op jit(solution)/shard_map/jit(_take)/gather | solution.py:72
  245.6 9.9 %gather_fusion.8 = f32[256,5632]{1,0:T(8,128)} fusion(f32[5632,256]{0,1:T(8,128)} %copy.19, s32[1024]{0:T(1024)S(1)} %pad_clamp_fusion.6), kind=kCustom, calls=%fused_computation.3.clone | custom fusion | bytes 11535360 | tf_op jit(solution)/shard_map/jit(_take)/gather | solution.py:73
  272.2 268.8 %all-gather.4.cloned.1.call-done = f32[5632,1024]{1,0:T(8,128)} async-done(((f32[5632,128]{1,0:T(8,128)}), f32[5632,1024]{1,0:T(8,128)}) %all-gather.4.cloned.1.call-update) | async-done | bytes 23068688 | tf_op jit(solution)/shard_map/all_gather | solution.py:80
  543.6 37.5 %all-gather.6.cloned.1.call-done = f32[2048,512]{1,0:T(8,128)} async-done(((f32[128,512]{1,0:T(8,128)}), f32[2048,512]{1,0:T(8,128)}) %all-gather.6.cloned.1.call-update) | async-done | bytes 4194320 | tf_op jit(solution)/shard_map/all_gather | solution.py:83
  585.8 11.7 %cholesky.103 = f32[128,128]{1,0:T(8,128)S(1)} custom-call(f32[128,128]{1,0:T(8,128)S(1)} %cholesky.263), custom_call_target="Cholesky" | custom-call | tf_op jit(solution)/shard_map/jit(cholesky)/cholesky | solution.py:30
  597.7 9.8 %custom-call.31 = f32[1,128,128]{1,2,0:T(8,128)S(1)} custom-call(f32[1,128,128]{2,1,0:T(8,128)S(1)} %get-tuple-element.48), custom_call_target="InvertDiagBlocksLowerTriangular" | custom-call | tf_op jit(solution)/shard_map/jit(cholesky)/cholesky | solution.py:30
  610.0 11.7 %cholesky.215 = f32[128,128]{1,0:T(8,128)S(1)} custom-call(f32[128,128]{1,0:T(8,128)S(1)} %cholesky.267), custom_call_target="Cholesky" | custom-call | tf_op jit(solution)/shard_map/jit(cholesky)/cholesky | solution.py:30
  623.2 9.9 %custom-call.32 = f32[1,128,128]{1,2,0:T(8,128)S(1)} custom-call(f32[1,128,128]{2,1,0:T(8,128)S(1)} %get-tuple-element.45), custom_call_target="InvertDiagBlocksLowerTriangular" | custom-call | tf_op jit(solution)/shard_map/jit(cholesky)/cholesky | solution.py:30
  634.7 11.7 %cholesky.236 = f32[128,128]{1,0:T(8,128)S(1)} custom-call(f32[128,128]{1,0:T(8,128)S(1)} %cholesky.272), custom_call_target="Cholesky" | custom-call | tf_op jit(solution)/shard_map/jit(cholesky)/cholesky | solution.py:30
  647.1 9.8 %custom-call.33 = f32[1,128,128]{1,2,0:T(8,128)S(1)} custom-call(f32[1,128,128]{2,1,0:T(8,128)S(1)} %get-tuple-element.42), custom_call_target="InvertDiagBlocksLowerTriangular" | custom-call | tf_op jit(solution)/shard_map/jit(cholesky)/cholesky | solution.py:30
  658.4 11.9 %cholesky.253 = f32[128,128]{1,0:T(8,128)S(1)} custom-call(f32[128,128]{1,0:T(8,128)S(1)} %convolution_subtract_fusion.5), custom_call_target="Cholesky" | custom-call | tf_op jit(solution)/shard_map/jit(cholesky)/cholesky | solution.py:30
  674.8 14.2 %while.1 = (s32[]{:T(128)}, f32[512,512]{1,0:T(8,128)}, s32[4,2]{0,1:T(2,128)S(1)}, f32[4,128,128]{2,1,0:T(8,128)}, s32[]{:T(128)}) while((s32[]{:T(128)}, f32[512,512]{1,0:T(8,128)}, s32[4,2]{0,1:T(2,128)S(1)}, f32[4,128,128]{2,1,0:T(8,128)}, s32[]{:T(128)}) %tuple.34), condition=%wide.while_cond, body=%wide.while_body.sunk | while | flops 2 | bytes 132705 | solution.py:31
  689.0 40.1 %custom-call.34 = f32[4,128,128]{1,2,0:T(8,128)S(1)} custom-call(f32[4,128,128]{2,1,0:T(8,128)} %get-tuple-element.26), custom_call_target="InvertDiagBlocksLowerTriangular" | custom-call | tf_op jit(solution)/shard_map/jit(_solve_triangular)/triangular_solve | solution.py:31
  736.6 15.3 %gather_fusion.2 = f32[5632,512]{1,0:T(8,128)} fusion(f32[512,512]{1,0:T(8,128)S(1)} %get-tuple-element.36, s32[6144]{0:T(1024)S(1)} %pad_clamp_fusion), kind=kCustom, calls=%fused_computation.6 | custom fusion | bytes 23091200 | tf_op jit(solution)/shard_map/jit(_take)/gather | solution.py:24
  751.9 24.2 %select_select_fusion = f32[5632,512]{1,0:T(8,128)S(1)} fusion(f32[5632,512]{1,0:T(8,128)} %gather_fusion.2, f32[5632,1024]{1,0:T(8,128)} %all-gather.4.cloned.1.call-done, pred[5632]{0:T(1024)(128)(4,1)S(1)} %get-tuple-element.51, pred[5632]{0:T(1024)(128)(4,1)S(1)} %get-tuple-element.52, f32[128,512]{1,0:T(8,128)S(1)} %fusion.40, ...), kind=kOutput, calls=%fused_computation.13 | convolution fusion | flops 17723293696 | bytes 35662848 | tf_op jit(solution)/shard_map/dot_general | solution.py:23
  781.3 12.2 %copy.23 = f32[5632,512]{0,1:T(8,128)} copy(f32[5632,512]{1,0:T(8,128)} %copy-done.1) | data formatting | bytes 23068672 | tf_op jit(solution)/shard_map/jit(_where)/select_n | solution.py:25
  793.5 11.8 %gather_fusion.3 = f32[256,5632]{1,0:T(8,128)} fusion(f32[5632,512]{0,1:T(8,128)} %copy.23, s32[1024]{0:T(1024)S(1)} %pad_clamp_fusion.5), kind=kCustom, calls=%fused_computation.7 | custom fusion | bytes 11535360 | tf_op jit(solution)/shard_map/jit(_take)/gather | solution.py:94
  822.0 16.7 %fusion.4 = f32[5632,256]{1,0:T(8,128)} fusion(f32[5632,256]{1,0:T(8,128)} %copy-done.2, f32[5632,512]{1,0:T(8,128)} %copy-done.1, f32[256,5632]{0,1:T(8,128)} %copy.24, pred[5632]{0:T(1024)(128)(4,1)S(1)} %get-tuple-element.52, pred[256]{0:T(512)(128)(4,1)S(1)} %get-tuple-element.56, pred[256]{0:T(512)(128)(4,1)S(1)} %broadcast_compare_fusion.1, ...), kind=kOutput, calls=%fused_computation.15 | convolution fusion | flops 8864268288 | bytes 29366528 | tf_op jit(solution)/shard_map/dot_general | solution.py:93
  (125 shorter events, 151.3 us)
Async XLA Ops:
  88.1 82.8 %copy-start = (s32[90112]{0:T(1024)S(1)}, s32[90112]{0:T(1024)}, u32[]{:S(2)}) copy-start(s32[90112]{0:T(1024)} %param.16) | copy-start | bytes 1081348
  88.1 120.4 %all-to-all-start = ((f32[352,128,32]{0,2,1:T(8,128)}), f32[352,128,32]{0,2,1:T(8,128)}, u32[]{:S(2)}, u32[]{:S(2)}) async-start(f32[352,128,32]{0,2,1:T(8,128)} %bitcast.76), calls=%async_computation | async-start | bytes 12582912 | tf_op jit(solution)/shard_map/all_to_all | solution.py:66
  99.3 441.8 %all-gather.4.cloned.1.call-start = ((), (), s32[]{:S(2)}) async-start(), calls=%async_computation.1 | async-start | bytes 25952256 | tf_op jit(solution)/shard_map/all_gather | solution.py:80
  255.5 6.3 copy-start.5
  267.8 2.5 copy-start.2
  272.2 308.9 %all-gather.6.cloned.1.call-start = ((), (), s32[]{:S(2)}) async-start(), calls=%async_computation.2 | async-start | bytes 4456448 | tf_op jit(solution)/shard_map/all_gather | solution.py:83
  542.8 275.9 %all-gather.8.cloned.1.call-start = ((), (), s32[]{:S(2)}) async-start(), calls=%async_computation.3 | async-start | bytes 4456448 | tf_op jit(solution)/shard_map/all_gather | solution.py:88
  584.8 1.0 copy-start.3
  729.2 1.5 copy-start.4
  776.1 4.4 copy-start.1
Sparse Core Ops, SparseCore 0:
  272.3 268.7 all-gather.3
  542.9 38.1 all-gather.5
  781.4 37.2 all-gather.7
where the time goes:
time: 853 us; the launch traced here: 846 us
  waiting for transfers between devices  313 us (37%)
  other arithmetic  250 us (29%)
  local copies, waits for them, and re-layouts  199 us (23%)
  matrix products  53.7 us (6%)
  between operations  17.9 us (2%)
  starting transfers between devices  11.7 us (1%)
    all_gather x1, waiting for transfers between devices, shards(): lax.all_gather(first_block, 'pcol', axis=1, tiled=True)[:, :PANEL]  269 us
    another operation x15, other arithmetic, cholesky_block(): factor = jnp.linalg.cholesky(symmetric)  79.5 us
    sort x2, other arithmetic, placement(): jnp.argsort(owners, stable=True)  76.5 us
    another operation x3, other arithmetic, cholesky_block(): jax.scipy.linalg.solve_triangular(factor, jnp.eye(PANEL, dtype=jnp.float3...  41.4 us
    all_gather x1, waiting for transfers between devices, shards(): lax.all_gather(panel_block[:BLOCK], 'prow', axis=0, tiled=True)  37.5 us
    gather x2, local copies, waits for them, and re-layouts, placement(): places = jnp.take(targets, sources) - device * amount  31.2 us
    dot_general x1, matrix products, factor_rows(): solved = jnp.dot(raw_rows, inverse.T, precision=lax.Precision.HIGHEST)  24.2 us
    gather x2, local copies, waits for them, and re-layouts, shards(): jnp.take(local_factors, jnp.minimum(order_cols, PANEL - 1), axis=1)  18.1 us
  transfers between devices with their start and end apart: 4, of which 3 were waited for; matrix products, arithmetic and copies ran while one was open for 16% of the time, Pallas kernels for 0%

commit v1 on v0

v1 whole, which is shorter than its diff:
```python
import functools

import jax
import jax.numpy as jnp
from jax import lax
from jax.experimental import pallas as pl
from jax.experimental.pallas import tpu as pltpu
from jax.sharding import PartitionSpec as P

F32, BF16 = jnp.float32, jnp.bfloat16
MESH = pl.DeviceIdType.MESH
HIGHEST = lax.Precision.HIGHEST
PANEL, BLOCK = 512, 128
NPR, NPC = 16, 8
RH, CH = 5632, 256
GR, GC = RH // NPR, CH // NPC
QR = GR // 4
CR = 256
NC = RH // CR
VMEM_LIMIT = 60 * 2**20


def iota(shape, dim):
    return lax.broadcasted_iota(jnp.int32, shape, dim)


def select_columns(values, onehot):
    high = values.astype(BF16)
    rest = values - high.astype(F32)
    middle = rest.astype(BF16)
    low = (rest - middle.astype(F32)).astype(BF16)
    dot = functools.partial(jnp.dot, preferred_element_type=F32)
    return dot(high, onehot) + dot(middle, onehot) + dot(low, onehot)


def regroup(parts, lane):
    results = []
    for m in range(4):
        joined = None
        for k in range(4):
            moved = parts[k] if k == m else pltpu.roll(parts[k], ((k - m) * GC) % 128, 1)
            joined = moved if k == 0 else jnp.where(lane // GC == k, moved, joined)
        results.append(joined)
    return results


def pack_kernel(order, col_down, col_across, x, out, rows, onehot):
    part = pl.program_id(0)

    @pl.when(part == 0)
    def _():
        below = (col_down[...] > col_across[...]).astype(F32)
        rank = jnp.sum(below, axis=1, keepdims=True).astype(jnp.int32)
        onehot[...] = jnp.where(rank == iota((CH, CH), 1), 1.0, 0.0).astype(BF16)

    base = part * GR

    def gather(i, carry):
        for u in range(8):
            rows[i, u : u + 1, :] = x[pl.ds(order[base + i * 8 + u], 1), :]
        return carry

    lax.fori_loop(0, GR // 8, gather, 0)
    picked = select_columns(rows[...].reshape(GR, CH), onehot[...])
    lane = iota((QR, 128), 1)
    for half in range(2):
        parts = [picked[g * QR : (g + 1) * QR, half * 128 : half * 128 + 128] for g in range(4)]
        for q, joined in enumerate(regroup(parts, lane)):
            out[half * 4 + q] = joined


def pack(order, col_targets, x):
    return pl.pallas_call(
        pack_kernel,
        out_shape=jax.ShapeDtypeStruct((NPR * NPC, QR, 128), F32),
        grid_spec=pltpu.PrefetchScalarGridSpec(
            num_scalar_prefetch=1,
            grid=(NPR,),
            in_specs=[
                pl.BlockSpec((CH, 1), lambda i, o: (0, 0)),
                pl.BlockSpec((1, CH), lambda i, o: (0, 0)),
                pl.BlockSpec((RH, CH), lambda i, o: (0, 0), pipeline_mode=pl.Buffered(1)),
            ],
            out_specs=pl.BlockSpec((NPC, QR, 128), lambda i, o: (i, 0, 0)),
            scratch_shapes=[pltpu.VMEM((GR // 8, 8, CH), F32), pltpu.VMEM((CH, CH), BF16)],
        ),
        compiler_params=pltpu.CompilerParams(vmem_limit_bytes=VMEM_LIMIT),
        name="pack",
    )(order, col_targets.reshape(CH, 1), col_targets.reshape(1, CH), x)


OUT_ROWS = 512


def unpack_kernel(place, weights, col_all, kaula, received, goce, out, moved, rows, onehot):
    step = pl.program_id(0)
    row_id, col_id = lax.axis_index("prow"), lax.axis_index("pcol")

    @pl.when(step == 0)
    def _():
        source = jnp.zeros((CH, 128), F32)
        here = col_id * CH + iota((CH, 128), 0)
        for r in range(16):
            source += jnp.where(col_all[r : r + 1, :] == here, float(r // 2), 0.0)
        source = jnp.sum(source, axis=1, keepdims=True)
        across = jnp.transpose(jnp.broadcast_to(source, (CH, 128)))[0:1, :]
        earlier = (source == across) & (iota((CH, CH), 0) < iota((CH, CH), 1))
        rank = jnp.sum(jnp.where(earlier, 1.0, 0.0), axis=0, keepdims=True)
        arrival = (across * GC + rank).astype(jnp.int32)
        onehot[...] = jnp.where(iota((CH, CH), 0) == arrival, 1.0, 0.0).astype(BF16)

    @pl.when(step < NPR)
    def _():
        lane = iota((QR, 128), 1)
        halves = [regroup([received[h * 4 + q] for q in range(4)], lane) for h in range(2)]
        joined = jnp.concatenate(
            [jnp.concatenate([halves[0][g], halves[1][g]], axis=1) for g in range(4)], axis=0
        )
        rows[...] = select_columns(joined, onehot[...]).reshape(GR // 8, 8, CH)
        base = step * GR

        def scatter(i, carry):
            for u in range(8):
                moved[pl.ds(place[base + i * 8 + u], 1), :] = rows[i, u : u + 1, :]
            return carry

        lax.fori_loop(0, GR // 8, scatter, 0)

    @pl.when(step >= NPR)
    def _():
        part = step - NPR
        first = pl.multiple_of(part * OUT_ROWS, OUT_ROWS)
        out[...] = weights[0] * moved[pl.ds(first, OUT_ROWS), :] + weights[1] * goce[...]

    @pl.when((step == NPR) & (row_id % NPC == col_id))
    def _():
        equal = iota((BLOCK, BLOCK), 0) == iota((BLOCK, BLOCK), 1)
        for half in range(2):
            cols = slice(half * BLOCK, (half + 1) * BLOCK)
            add = jnp.where(equal & (row_id // NPC == half), kaula[:, cols], 0.0)
            out[:BLOCK, cols] = out[:BLOCK, cols] + add


def unpack(place, weights, col_all, kaula, received, goce):
    return pl.pallas_call(
        unpack_kernel,
        out_shape=jax.ShapeDtypeStruct((RH, CH), F32),
        grid_spec=pltpu.PrefetchScalarGridSpec(
            num_scalar_prefetch=2,
            grid=(NPR + RH // OUT_ROWS,),
            in_specs=[
                pl.BlockSpec((16, 128), lambda i, *_: (0, 0)),
                pl.BlockSpec((1, CH), lambda i, *_: (0, 0)),
                pl.BlockSpec((NPC, QR, 128), lambda i, *_: (jnp.minimum(i, NPR - 1), 0, 0)),
                pl.BlockSpec((OUT_ROWS, CH), lambda i, *_: (jnp.maximum(i - NPR, 0), 0)),
            ],
            out_specs=pl.BlockSpec((OUT_ROWS, CH), lambda i, *_: (jnp.maximum(i - NPR, 0), 0)),
            scratch_shapes=[
                pltpu.VMEM((RH, CH), F32),
                pltpu.VMEM((GR // 8, 8, CH), F32),
                pltpu.VMEM((CH, CH), BF16),
            ],
        ),
        compiler_params=pltpu.CompilerParams(vmem_limit_bytes=VMEM_LIMIT),
        name="unpack",
    )(place, weights, col_all.reshape(16, 128), kaula.reshape(1, CH), received, goce)


def eliminate(group, carry, factor_t, inverse):
    d, x = list(carry[:16]), list(carry[16:])
    lane, sub = iota((8, 128), 1), iota((8, 128), 0)
    f_rows = jnp.zeros((8, 128), F32)
    x_rows = jnp.zeros((8, 128), F32)
    live = lane < 128 - 8 * group
    for s in range(8):
        row = jnp.broadcast_to(d[0][s : s + 1, :], (8, 128))
        pivot = jnp.broadcast_to(row[:, s : s + 1], (8, 128))
        r = lax.rsqrt(pivot)
        r = r * (1.5 - 0.5 * pivot * r * r)
        row = jnp.where(live & (lane >= s), row, 0.0) * r
        x_row = jnp.broadcast_to(x[0][s : s + 1, :], (8, 128)) * r
        f_rows = jnp.where(sub == s, row, f_rows)
        x_rows = jnp.where(sub == s, x_row, x_rows)
        row, x_row = row * r, x_row * r
        for i in range(16):
            column = jnp.broadcast_to(d[i][:, s : s + 1], (8, 128))
            d[i] = d[i] - column * row
            x[i] = x[i] - column * x_row
        d[0] = jnp.where(sub == s, 0.0, d[0])
    at = pl.ds(pl.multiple_of(group * 8, 8), 8)
    factor_t[at, :] = pltpu.roll(f_rows, group * 8, 1)
    inverse[at, :] = x_rows
    d = [pltpu.roll(v, 120, 1) for v in d[1:] + d[:1]]
    return tuple(d + x[1:] + x[:1])


def panel_kernel(
    a_hbm, out, a, panel, heads, work, factor_t, w_high, w_low, diag_f, diag_x,
    load, sent0, got0, sent1, got1, sent2, got2, head_sent, head_got,
):
    row_id, col_id = lax.axis_index("prow"), lax.axis_index("pcol")
    cx, cy = col_id // 2, col_id % 2
    cz, cyc = row_id // 4, row_id % 4
    left = cx < 2
    b = jnp.where(left, cx, 3 - cx)
    own = b * 2 + cy
    cross = (row_id, (3 - cx) * 2 + cy)
    x_mate = (row_id, (cx + 1 - 2 * (cx % 2)) * 2 + cy)
    y_mate = (row_id, cx * 2 + 1 - cy)
    over_z = [(lax.rem(cz + k, 4) * 4 + cyc, col_id) for k in (1, 2, 3)]
    in_z = [(cz * 4 + lax.rem(cyc + k, 4), col_id) for k in (1, 2, 3)]

    @pl.when(left)
    def _():
        pltpu.make_async_copy(a_hbm.at[:, pl.ds(0, BLOCK)], panel.at[own], load.at[0]).start()

    pltpu.make_async_copy(a_hbm, a, load.at[1]).start()
    barrier = pltpu.get_barrier_semaphore()
    for device in [cross, x_mate, y_mate] + over_z + in_z:
        pl.semaphore_signal(barrier, inc=1, device_id=device, device_id_type=MESH)
    pl.semaphore_wait(barrier, 9)

    @pl.when(left)
    def _():
        pltpu.make_async_copy(a_hbm.at[:, pl.ds(0, BLOCK)], panel.at[own], load.at[0]).wait()

    def piece(j, c):
        return panel.at[j, pl.ds(c * CR, CR), :]

    def send(j, c, sent, got, device):
        return pltpu.make_async_remote_copy(
            piece(j, c), piece(j, c), sent, got, device_id=device, device_id_type=MESH
        )

    flip_x, flip_y = (1 - b) * 2 + cy, b * 2 + 1 - cy
    flip_both = (1 - b) * 2 + 1 - cy

    def plan(c):
        if c % 2 == 0:
            return x_mate, flip_x, y_mate, flip_y
        return y_mate, flip_y, x_mate, flip_x

    def start0(c):
        @pl.when(left)
        def _():
            send(own, c, sent0.at[c], got0.at[c], cross).start()

    def start1(c):
        @pl.when(jnp.logical_not(left))
        def _():
            send(own, c, sent0.at[c], got0.at[c], cross).wait_recv()

        send(own, c, sent1.at[c], got1.at[c], plan(c)[0]).start()

    def start2(c):
        mate1, j1, mate2, _ = plan(c)
        send(j1, c, sent1.at[c], got1.at[c], mate1).wait_recv()
        send(own, c, sent2.at[c, 0], got2.at[c, 0], mate2).start()
        send(j1, c, sent2.at[c, 1], got2.at[c, 1], mate2).start()

    def finish2(c):
        _, _, mate2, j2 = plan(c)
        send(j2, c, sent2.at[c, 0], got2.at[c, 0], mate2).wait_recv()
        send(flip_both, c, sent2.at[c, 1], got2.at[c, 1], mate2).wait_recv()

    ahead0, ahead1 = 6, 3

    def tick(t):
        if t + ahead0 < NC:
            start0(t + ahead0)
        if t + ahead1 < NC:
            start1(t + ahead1)
        if t < NC:
            start2(t)

    for c in range(ahead0):
        start0(c)
    for c in range(ahead1):
        start1(c)

    head = panel.at[:, pl.ds(0, BLOCK), :]
    a_owner = cyc == col_id % 4
    first_z = col_id // 4

    def head_local(slot):
        return pltpu.make_async_copy(head, heads.at[slot], head_got.at[slot])

    def head_copy(source, slot, k, base, device):
        return pltpu.make_async_remote_copy(
            source, heads.at[slot], head_sent.at[base + k], head_got.at[slot],
            device_id=device, device_id_type=MESH,
        )

    sources = [(cz == 0, cyc, 0), (a_owner & (cz == first_z), 4, 3), (a_owner & (cz == first_z + 2), 5, 6)]

    def head_out():
        for mine, slot, base in sources:

            @pl.when(mine)
            def _(slot=slot, base=base):
                head_local(slot).start()
                for k in range(3):
                    head_copy(head, slot, k, base, over_z[k]).start()

    def head_spread():
        head_local(cyc).wait()
        for k in range(3):
            head_copy(heads.at[cyc], cyc, k, 9, in_z[k]).start()

        @pl.when(a_owner)
        def _():
            for slot, base in ((4, 12), (5, 15)):
                head_local(slot).wait()
                for k in range(3):
                    head_copy(heads.at[slot], slot, k, base, in_z[k]).start()

    def head_in():
        for k in (1, 2, 3):
            head_local(lax.rem(cyc + k, 4)).wait()

        @pl.when(jnp.logical_not(a_owner))
        def _():
            for slot in (4, 5):
                head_local(slot).wait()

    def head_done():
        for mine, slot, base in sources:

            @pl.when(mine)
            def _(slot=slot, base=base):
                for k in range(3):
                    head_copy(head, slot, k, base, over_z[k]).wait_send()

        for k in range(3):
            head_copy(heads.at[cyc], cyc, k, 9, in_z[k]).wait_send()

        @pl.when(a_owner)
        def _():
            for slot, base in ((4, 12), (5, 15)):
                for k in range(3):
                    head_copy(heads.at[slot], slot, k, base, in_z[k]).wait_send()

    t = 0

    def advance():
        nonlocal t
        tick(t)
        t += 1

    advance()
    advance()
    finish2(0)
    head_out()
    advance()
    advance()
    head_spread()
    advance()
    advance()
    head_in()

    lower = iota((BLOCK, BLOCK), 0) >= iota((BLOCK, BLOCK), 1)
    for i in range(4):
        rows = slice(i * BLOCK, (i + 1) * BLOCK)
        for j in range(i):
            block = heads[i, j]
            work[rows, j * BLOCK : (j + 1) * BLOCK] = block
            work[j * BLOCK : (j + 1) * BLOCK, rows] = jnp.transpose(block)
        block = heads[i, i]
        work[rows, rows] = jnp.where(lower, block, jnp.transpose(block))
        for j in range(4):
            unit = jnp.where(iota((BLOCK, BLOCK), 0) == iota((BLOCK, BLOCK), 1), float(i == j), 0.0)
            work[rows, PANEL + j * BLOCK : PANEL + (j + 1) * BLOCK] = unit
            factor_t[rows, j * BLOCK : (j + 1) * BLOCK] = jnp.zeros((BLOCK, BLOCK), F32)

    for k in range(4):
        rows = slice(k * BLOCK, (k + 1) * BLOCK)
        carry = [work[k * BLOCK + g * 8 : k * BLOCK + g * 8 + 8, rows] for g in range(16)]
        carry += [
            work[k * BLOCK + g * 8 : k * BLOCK + g * 8 + 8, PANEL + k * BLOCK : PANEL + (k + 1) * BLOCK]
            for g in range(16)
        ]
        carry = tuple(carry)
        for part in range(4):
            carry = lax.fori_loop(
                part * 4, part * 4 + 4, lambda g, v: eliminate(g, v, diag_f, diag_x), carry
            )
            if part % 2:
                advance()
        factor_t[rows, rows] = diag_f[...]
        right = (k + 1) * BLOCK
        width = PANEL + (k + 1) * BLOCK - right
        solved = jnp.dot(diag_x[...], work[rows, right : right + width], precision=HIGHEST)
        work[rows, right : right + width] = solved
        count = PANEL - right
        if count:
            factor_t[rows, right:PANEL] = solved[:, :count]
            turned = jnp.transpose(solved[:, :count])
            work[right:PANEL, right : right + width] -= jnp.dot(turned, solved, precision=HIGHEST)
        advance()

    columns = jnp.concatenate(
        [jnp.concatenate([heads[4 + i, j] for j in range(4)], axis=1) for i in range(2)], axis=0
    )
    solved = lax.dot_general(
        work[:, PANEL:], columns, (((1,), (1,)), ((), ())), precision=HIGHEST, preferred_element_type=F32
    )
    turned = jnp.transpose(work[:, PANEL:])
    weight = jnp.dot(turned, solved, precision=HIGHEST)
    work[:, :PANEL] = turned
    own_panel = col_id < PANEL // BLOCK
    direct = -work[:, pl.ds(pl.multiple_of(jnp.minimum(col_id, 3) * BLOCK, BLOCK), BLOCK)]
    weight = jnp.concatenate([jnp.where(own_panel, direct, weight[:, :BLOCK]), weight[:, BLOCK:]], axis=1)
    high = weight.astype(BF16)
    w_high[...] = high
    w_low[...] = (weight - high.astype(F32)).astype(BF16)
    while t < NC:
        advance()

    pltpu.make_async_copy(a_hbm, a, load.at[1]).wait()
    in_panel = iota((CR, CH), 1) < jnp.where(own_panel, BLOCK, 0)
    dot = functools.partial(jnp.dot, preferred_element_type=F32)
    for c in range(NC):
        if c:
            finish2(c)
        at = slice(c * CR, (c + 1) * CR)
        left_rows = jnp.concatenate([panel[j, at, :] for j in range(4)], axis=1)
        high = left_rows.astype(BF16)
        low = (left_rows - high.astype(F32)).astype(BF16)
        update = dot(high, w_high[...]) + (dot(high, w_low[...]) + dot(low, w_high[...]))
        out[at, :] = jnp.where(in_panel, 0.0, a[at, :]) - update
        if c == 0:

            @pl.when(row_id < PANEL // BLOCK)
            def _():
                d, j = jnp.minimum(row_id, 3), jnp.minimum(col_id, 3)
                block = factor_t[
                    pl.ds(pl.multiple_of(j * BLOCK, BLOCK), BLOCK), pl.ds(pl.multiple_of(d * BLOCK, BLOCK), BLOCK)
                ]
                out[:BLOCK, :BLOCK] = jnp.where(own_panel, jnp.transpose(block), a[:BLOCK, :BLOCK])
                out[:BLOCK, BLOCK:] = a[:BLOCK, BLOCK:]

    for c in range(NC):

        @pl.when(left)
        def _(c=c):
            send(own, c, sent0.at[c], got0.at[c], cross).wait_send()

        mate1, j1, mate2, _ = plan(c)
        send(own, c, sent1.at[c], got1.at[c], mate1).wait_send()
        send(own, c, sent2.at[c, 0], got2.at[c, 0], mate2).wait_send()
        send(j1, c, sent2.at[c, 1], got2.at[c, 1], mate2).wait_send()
    head_done()


def panel_step(combined):
    dma = pltpu.SemaphoreType.DMA
    return pl.pallas_call(
        panel_kernel,
        out_shape=jax.ShapeDtypeStruct((RH, CH), F32),
        in_specs=[pl.BlockSpec(memory_space=pl.ANY)],
        out_specs=pl.BlockSpec(memory_space=pltpu.VMEM),
        scratch_shapes=[
            pltpu.VMEM((RH, CH), F32),
            pltpu.VMEM((4, RH, BLOCK), F32),
            pltpu.VMEM((6, 4, BLOCK, BLOCK), F32),
            pltpu.VMEM((PANEL, 2 * PANEL), F32),
            pltpu.VMEM((PANEL, PANEL), F32),
            pltpu.VMEM((PANEL, CH), BF16),
            pltpu.VMEM((PANEL, CH), BF16),
            pltpu.VMEM((BLOCK, BLOCK), F32),
            pltpu.VMEM((BLOCK, BLOCK), F32),
            dma((2,)),
            dma((NC,)),
            dma((NC,)),
            dma((NC,)),
            dma((NC,)),
            dma((NC, 2)),
            dma((NC, 2)),
            dma((18,)),
            dma((6,)),
        ],
        compiler_params=pltpu.CompilerParams(
            collective_id=0, has_side_effects=True, vmem_limit_bytes=VMEM_LIMIT
        ),
        name="panel_step",
    )(combined)


def shards(grace_slab, goce_slab, grace_weight, goce_weight, kaula_prior, row_target, column_target):
    row_id, col_id = lax.axis_index("prow"), lax.axis_index("pcol")
    targets = lax.dynamic_slice_in_dim(row_target, row_id * RH, RH)
    targets, order = lax.sort((targets, jnp.arange(RH, dtype=jnp.int32)), num_keys=1)
    place = lax.all_to_all(targets.reshape(NPR, GR), "prow", split_axis=0, concat_axis=0, tiled=True)
    place = place.reshape(RH) - row_id * RH
    col_targets = lax.dynamic_slice_in_dim(column_target, col_id * CH, CH)
    packed = pack(order, col_targets, grace_slab)
    received = lax.all_to_all(packed, ("prow", "pcol"), split_axis=0, concat_axis=0, tiled=True)
    weights = jnp.concatenate([grace_weight, goce_weight])
    combined = unpack(place, weights, column_target, kaula_prior, received, goce_slab)
    return panel_step(combined)


def solution(mesh):
    return jax.shard_map(
        shards,
        mesh=mesh,
        in_specs=(P("prow", "pcol"), P("prow", "pcol"), P(), P(), P("pcol"), P(), P()),
        out_specs=P("prow", "pcol"),
        check_vma=False,
    )
```

time: 853 us -> 336 us (0.39)
  waiting for transfers between devices: 313 us -> 65.2 us
  other arithmetic: 250 us -> 7.47 us
  Pallas kernels: 0 us -> 235 us
  local copies, waits for them, and re-layouts: 199 us -> 9.28 us
  matrix products: 53.7 us -> 0 us
  between operations: 17.9 us -> 1.32 us
    all_gather x3 -> x0, waiting for transfers between devices: 313 us -> none  [the longest x1 269 us: shards(): lax.all_gather(first_block, 'pcol', axis=1, tiled=True)[:, :PANEL]]
    pallas_call x0 -> x3, Pallas kernels: none -> 235 us  [the longest x1 170 us: panel_step(): pl.pallas_call(panel_kernel, out_shape=jax.ShapeDtypeStruct((RH, CH), F32...]
    gather x11 -> x0, local copies, waits for them, and re-layouts: 128 us -> none  [the longest x2 31.2 us: placement(): places = jnp.take(targets, sources) - device * amount]
    another operation x18 -> x0, other arithmetic: 121 us -> none  [the longest x15 79.5 us: cholesky_block(): factor = jnp.linalg.cholesky(symmetric)]
    sort x6 -> x1, other arithmetic: 96.4 us -> 6.76 us  [shards(): lax.sort((targets, jnp.arange(RH, dtype=jnp.int32)), num_keys=1)]
    all_to_all x1 -> x2, waiting for transfers between devices: 0.01 us -> 65.2 us  [the longest x1 65.2 us: shards(): lax.all_to_all(packed, ('prow', 'pcol'), split_axis=0, concat_axis=0, til...]
    dot_general x2 -> x0, matrix products: 40.9 us -> none  [the longest x1 24.2 us: factor_rows(): solved = jnp.dot(raw_rows, inverse.T, precision=lax.Precision.HIGHEST)]
    select_n x5 -> x0, local copies, waits for them, and re-layouts: 31.3 us -> none  [the longest x1 12.2 us: factor_rows(): return jnp.where(order_rows[:, None] < PANEL, known, solved)]
  transfers between devices with their start and end apart: 4 -> 2, of which waited for: 3 -> 1; matrix products, arithmetic and copies ran while one was open for 16% -> 1% of each run, Pallas kernels for 0% -> 9%
where the time goes in v1:
time: 336 us; the launch traced here: 335 us
  Pallas kernels  235 us (70%)
  waiting for transfers between devices  65.2 us (19%)
  starting transfers between devices  16.7 us (5%)
  local copies, waits for them, and re-layouts  9.28 us (3%)
  other arithmetic  7.47 us (2%)
    pallas_call x1, Pallas kernels, panel_step(): pl.pallas_call(panel_kernel, out_shape=jax.ShapeDtypeStruct((RH, CH), F32...  170 us
    all_to_all x1, waiting for transfers between devices, shards(): lax.all_to_all(packed, ('prow', 'pcol'), split_axis=0, concat_axis=0, til...  65.2 us
    pallas_call x1, Pallas kernels, unpack(): pl.pallas_call(unpack_kernel, out_shape=jax.ShapeDtypeStruct((RH, CH), F3...  35.6 us
    pallas_call x1, Pallas kernels, pack(): pl.pallas_call(pack_kernel, out_shape=jax.ShapeDtypeStruct((NPR * NPC, QR...  29.5 us
    all_to_all x1, starting transfers between devices, shards(): lax.all_to_all(packed, ('prow', 'pcol'), split_axis=0, concat_axis=0, til...  9.69 us
    all_to_all x1, starting transfers between devices, shards(): lax.all_to_all(targets.reshape(NPR, GR), 'prow', split_axis=0, concat_axi...  7.01 us
    sort x1, other arithmetic, shards(): lax.sort((targets, jnp.arange(RH, dtype=jnp.int32)), num_keys=1)  6.76 us
  transfers between devices with their start and end apart: 2, of which 1 were waited for; matrix products, arithmetic and copies ran while one was open for 1% of the time, Pallas kernels for 9%

profile of v1, /device:TPU:7, one launch (start us, length us, event | category | flops | bytes accessed | tf_op | source)
XLA Modules:
  0.0 335.4 jit_solution(169542208684627156)
XLA Ops:
  0.0 0.8 dynamic_slice.6
  0.8 6.8 %sort.15 = (s32[5632]{0:T(1024)S(1)}, s32[5632]{0:T(1024)}) sort(s32[5632]{0:T(1024)S(1)} %dynamic_slice.6, s32[5632]{0:T(1024)S(1)} %iota.3), dimensions={0}, to_apply=%region_0.0 | sort | flops 73216 | bytes 90112 | tf_op jit(solution)/shard_map/sort | solution.py:492
  7.6 0.7 all_to_all.9
  8.3 7.0 %all-to-all-start = ((s32[16,1,352]{2,1,0:T(1,128)}), s32[16,1,352]{2,1,0:T(1,128)S(1)}, u32[]{:S(2)}, u32[]{:S(2)}) async-start(s32[16,1,352]{2,1,0:T(1,128)} %all_to_all.9), calls=%async_computation | async-start | bytes 49152 | tf_op jit(solution)/shard_map/all_to_all | solution.py:493
  15.3 0.8 dynamic_slice.7
  16.1 0.0 copy-start
  16.1 0.8 copy.8.col_down
  16.8 0.0 copy-done
  16.8 29.5 %pack.1 = f32[128,88,128]{2,1,0:T(8,128)} custom-call(s32[5632]{0:T(1024)} %get-tuple-element.8.order, s32[256,1]{1,0:T(8,128)} %copy.8.col_down, s32[1,256]{1,0:T(1,128)} %bitcast.6, f32[5632,256]{1,0:T(8,128)} %x.1), custom_call_target="tpu_custom_call" | custom-call | tf_op jit(solution)/shard_map/pack/pallas_call | solution.py:73
  46.3 0.0 all-to-all-done
  46.3 9.7 %all-to-all-start.1 = ((f32[128,88,128]{2,1,0:T(8,128)}), f32[128,88,128]{2,1,0:T(8,128)}, u32[]{:S(2)}, u32[]{:S(2)}) async-start(f32[128,88,128]{2,1,0:T(8,128)} %pack.1), calls=%async_computation.1 | async-start | bytes 11534336 | tf_op jit(solution)/shard_map/all_to_all | solution.py:497
  57.3 0.6 pad_maximum_fusion.weights
  57.9 0.1 subtract_reduce_fusion
  58.0 0.7 sub.10.place
  58.7 65.2 %all-to-all-done.1.received = f32[128,88,128]{2,1,0:T(8,128)} async-done(((f32[128,88,128]{2,1,0:T(8,128)}), f32[128,88,128]{2,1,0:T(8,128)}, u32[]{:S(2)}, u32[]{:S(2)}) %all-to-all-start.1) | async-done | bytes 5767200 | tf_op jit(solution)/shard_map/all_to_all | solution.py:497
  123.9 35.6 %unpack.1.a_hbm = f32[5632,256]{1,0:T(8,128)} custom-call(s32[5632]{0:T(1024)} %sub.10.place, f32[2]{0:T(128)} %pad_maximum_fusion.weights, s32[16,128]{1,0:T(8,128)} %bitcast.4, f32[1,256]{1,0:T(1,128)} %bitcast.7, f32[128,88,128]{2,1,0:T(8,128)} %all-to-all-done.1.received, f32[5632,256]{1,0:T(8,128)} %goce.1), custom_call_target="tpu_custom_call" | custom-call | tf_op jit(solution)/shard_map/unpack/pallas_call | solution.py:145
  159.5 170.3 %panel_step.1 = f32[5632,256]{1,0:T(8,128)} custom-call(f32[5632,256]{1,0:T(8,128)} %unpack.1.a_hbm), custom_call_target="tpu_custom_call" | custom-call | tf_op jit(solution)/shard_map/panel_step/pallas_call | solution.py:457
  329.8 5.5 %copy.12 = f32[5632,256]{1,0:T(8,128)} copy(f32[5632,256]{1,0:T(8,128)} %panel_step.1) | data formatting | bytes 11534336
  (1 shorter events, 0.0 us)
Async XLA Ops:
  8.3 38.0 %all-to-all-start = ((s32[16,1,352]{2,1,0:T(1,128)}), s32[16,1,352]{2,1,0:T(1,128)S(1)}, u32[]{:S(2)}, u32[]{:S(2)}) async-start(s32[16,1,352]{2,1,0:T(1,128)} %all_to_all.9), calls=%async_computation | async-start | bytes 49152 | tf_op jit(solution)/shard_map/all_to_all | solution.py:493
  16.1 0.8 copy-start
  46.3 77.6 %all-to-all-start.1 = ((f32[128,88,128]{2,1,0:T(8,128)}), f32[128,88,128]{2,1,0:T(8,128)}, u32[]{:S(2)}, u32[]{:S(2)}) async-start(f32[128,88,128]{2,1,0:T(8,128)} %pack.1), calls=%async_computation.1 | async-start | bytes 11534336 | tf_op jit(solution)/shard_map/all_to_all | solution.py:497

commit v2 on v1

--- a/solution.py
+++ b/solution.py
@@ -44,93 +44,209 @@
     return results
 
 
-def pack_kernel(order, col_down, col_across, x, out, rows, onehot):
-    part = pl.program_id(0)
-
-    @pl.when(part == 0)
-    def _():
-        below = (col_down[...] > col_across[...]).astype(F32)
-        rank = jnp.sum(below, axis=1, keepdims=True).astype(jnp.int32)
-        onehot[...] = jnp.where(rank == iota((CH, CH), 1), 1.0, 0.0).astype(BF16)
-
-    base = part * GR
-
-    def gather(i, carry):
-        for u in range(8):
-            rows[i, u : u + 1, :] = x[pl.ds(order[base + i * 8 + u], 1), :]
+def linear(row):
+    return row // 8 * 16 + row % 8
+
+
+def other_row(row_id, step, sign):
+    z, y, core = row_id // 4, row_id // 2 % 2, row_id % 2
+    dz, dy, dcore = step % 4, step // 4 % 2, step // 8
+    return lax.rem(z + sign * dz + 4, 4) * 4 + lax.rem(y + dy, 2) * 2 + lax.rem(core + dcore, 2)
+
+
+def other_col(col_id, step, sign):
+    x, y = col_id // 2, col_id % 2
+    return lax.rem(x + sign * (step // 2) + 4, 4) * 2 + lax.rem(y + step % 2, 2)
+
+
+def exchange_kernel(
+    order, col_down, col_across, col_all, places, x, out, places_out,
+    rows, packed, received, pick_out, pick_in, sent, got, place_sent, place_got,
+):
+    row_id, col_id = lax.axis_index("prow"), lax.axis_index("pcol")
+    me = row_id * NPC + col_id
+    lane = iota((QR, 128), 1)
+
+    barrier = pltpu.get_barrier_semaphore()
+
+    def greet(k, carry):
+        device = (other_row(row_id, k // NPC, 1), other_col(col_id, k % NPC, 1))
+        pl.semaphore_signal(barrier, inc=1, device_id=device, device_id_type=MESH)
         return carry
 
-    lax.fori_loop(0, GR // 8, gather, 0)
-    picked = select_columns(rows[...].reshape(GR, CH), onehot[...])
-    lane = iota((QR, 128), 1)
-    for half in range(2):
-        parts = [picked[g * QR : (g + 1) * QR, half * 128 : half * 128 + 128] for g in range(4)]
-        for q, joined in enumerate(regroup(parts, lane)):
-            out[half * 4 + q] = joined
-
-
-def pack(order, col_targets, x):
-    return pl.pallas_call(
-        pack_kernel,
-        out_shape=jax.ShapeDtypeStruct((NPR * NPC, QR, 128), F32),
-        grid_spec=pltpu.PrefetchScalarGridSpec(
-            num_scalar_prefetch=1,
-            grid=(NPR,),
-            in_specs=[
-                pl.BlockSpec((CH, 1), lambda i, o: (0, 0)),
-                pl.BlockSpec((1, CH), lambda i, o: (0, 0)),
-                pl.BlockSpec((RH, CH), lambda i, o: (0, 0), pipeline_mode=pl.Buffered(1)),
-            ],
-            out_specs=pl.BlockSpec((NPC, QR, 128), lambda i, o: (i, 0, 0)),
-            scratch_shapes=[pltpu.VMEM((GR // 8, 8, CH), F32), pltpu.VMEM((CH, CH), BF16)],
-        ),
-        compiler_params=pltpu.CompilerParams(vmem_limit_bytes=VMEM_LIMIT),
-        name="pack",
-    )(order, col_targets.reshape(CH, 1), col_targets.reshape(1, CH), x)
-
-
-OUT_ROWS = 512
-
-
-def unpack_kernel(place, weights, col_all, kaula, received, goce, out, moved, rows, onehot):
-    step = pl.program_id(0)
-    row_id, col_id = lax.axis_index("prow"), lax.axis_index("pcol")
-
-    @pl.when(step == 0)
-    def _():
-        source = jnp.zeros((CH, 128), F32)
-        here = col_id * CH + iota((CH, 128), 0)
-        for r in range(16):
-            source += jnp.where(col_all[r : r + 1, :] == here, float(r // 2), 0.0)
-        source = jnp.sum(source, axis=1, keepdims=True)
-        across = jnp.transpose(jnp.broadcast_to(source, (CH, 128)))[0:1, :]
-        earlier = (source == across) & (iota((CH, CH), 0) < iota((CH, CH), 1))
-        rank = jnp.sum(jnp.where(earlier, 1.0, 0.0), axis=0, keepdims=True)
-        arrival = (across * GC + rank).astype(jnp.int32)
-        onehot[...] = jnp.where(iota((CH, CH), 0) == arrival, 1.0, 0.0).astype(BF16)
-
-    @pl.when(step < NPR)
-    def _():
-        lane = iota((QR, 128), 1)
-        halves = [regroup([received[h * 4 + q] for q in range(4)], lane) for h in range(2)]
+    lax.fori_loop(1, NPR * NPC, greet, 0)
+
+    below = (col_down[...] > col_across[...]).astype(F32)
+    rank = jnp.sum(below, axis=1, keepdims=True).astype(jnp.int32)
+    pick_out[...] = jnp.where(rank == iota((CH, CH), 1), 1.0, 0.0).astype(BF16)
+
+    def pack(step):
+        dest = other_row(row_id, step, 1)
+        base = dest * GR
+
+        def gather(i, carry):
+            for u in range(16):
+                at = order[base + i * 16 + u]
+                tile, sub = i * 2 + u // 8, u % 8
+                rows[tile, 0, sub : sub + 1, :] = x[pl.ds(at, 1), :]
+                rows[tile, 1, sub : sub + 1, :] = x[pl.ds(at + 8, 1), :]
+            return carry
+
+        lax.fori_loop(0, GR // 16, gather, 0)
+        taken = jnp.concatenate([rows[:, h].reshape(GR, 128) for h in range(2)], axis=1)
+        picked = select_columns(taken, pick_out[...])
+        for half in range(2):
+            parts = [picked[g * QR : (g + 1) * QR, half * 128 : half * 128 + 128] for g in range(4)]
+            for q, joined in enumerate(regroup(parts, lane)):
+                packed[dest * NPC + half * 4 + q] = joined
+
+    def chunk_copy(dest_row, dest_col, source):
+        to = dest_row * NPC + dest_col
+        return pltpu.make_async_remote_copy(
+            packed.at[to], received.at[source], sent.at[to], got.at[source],
+            device_id=(dest_row, dest_col), device_id_type=MESH,
+        )
+
+    def place_copy(dest_row, source_row):
+        return pltpu.make_async_remote_copy(
+            places.at[dest_row], places_out.at[source_row], place_sent.at[dest_row],
+            place_got.at[source_row], device_id=(dest_row, col_id), device_id_type=MESH,
+        )
+
+    def own_copy():
+        return pltpu.make_async_copy(packed.at[me], received.at[me], got.at[me])
+
+    def own_places():
+        return pltpu.make_async_copy(places.at[row_id], places_out.at[row_id], place_got.at[row_id])
+
+    pack(0)
+    pl.semaphore_wait(barrier, NPR * NPC - 1)
+    pack(1)
+    own_copy().start()
+    own_places().start()
+    for k in range(1, NPC):
+        chunk_copy(row_id, other_col(col_id, k, 1), me).start()
+
+    def forward(step, carry):
+        @pl.when(step < NPR - 1)
+        def _():
+            pack(step + 1)
+
+        dest = other_row(row_id, step, 1)
+        place_copy(dest, row_id).start()
+        for k in range(NPC):
+            chunk_copy(dest, other_col(col_id, k, 1), me).start()
+        return carry
+
+    lax.fori_loop(1, NPR, forward, 0)
+
+    source = jnp.zeros((CH, 128), F32)
+    here = col_id * CH + iota((CH, 128), 0)
+    for r in range(16):
+        source += jnp.where(col_all[r : r + 1, :] == here, float(r // 2), 0.0)
+    source = jnp.sum(source, axis=1, keepdims=True)
+    across = jnp.transpose(jnp.broadcast_to(source, (CH, 128)))[0:1, :]
+    earlier = (source == across) & (iota((CH, CH), 0) < iota((CH, CH), 1))
+    rank = jnp.sum(jnp.where(earlier, 1.0, 0.0), axis=0, keepdims=True)
+    arrival = (across * GC + rank).astype(jnp.int32)
+    pick_in[...] = jnp.where(iota((CH, CH), 0) == arrival, 1.0, 0.0).astype(BF16)
+
+    def unpack(origin):
+        halves = [regroup([received[origin * NPC + h * 4 + q] for q in range(4)], lane) for h in range(2)]
         joined = jnp.concatenate(
             [jnp.concatenate([halves[0][g], halves[1][g]], axis=1) for g in range(4)], axis=0
         )
-        rows[...] = select_columns(joined, onehot[...]).reshape(GR // 8, 8, CH)
-        base = step * GR
+        picked = select_columns(joined, pick_in[...])
+        for h in range(2):
+            out[origin, :, h] = picked[:, h * 128 : h * 128 + 128].reshape(GR // 8, 8, 128)
+
+    own_copy().wait()
+    own_places().wait()
+    for k in range(1, NPC):
+        origin = other_col(col_id, k, -1)
+        chunk_copy(row_id, col_id, row_id * NPC + origin).wait_recv()
+    unpack(row_id)
+
+    def arrive(step, carry):
+        origin = other_row(row_id, step, -1)
+        place_copy(row_id, origin).wait_recv()
+        for k in range(NPC):
+            chunk_copy(row_id, col_id, origin * NPC + other_col(col_id, k, -1)).wait_recv()
+        unpack(origin)
+        return carry
+
+    lax.fori_loop(1, NPR, arrive, 0)
+
+    for k in range(1, NPC):
+        chunk_copy(row_id, other_col(col_id, k, 1), me).wait_send()
+
+    def leave(step, carry):
+        dest = other_row(row_id, step, 1)
+        place_copy(dest, row_id).wait_send()
+        for k in range(NPC):
+            chunk_copy(dest, other_col(col_id, k, 1), me).wait_send()
+        return carry
+
+    lax.fori_loop(1, NPR, leave, 0)
+
+
+def exchange(order, col_targets, col_all, places, x):
+    dma, vmem = pltpu.SemaphoreType.DMA, pl.BlockSpec(memory_space=pltpu.VMEM)
+    return pl.pallas_call(
+        exchange_kernel,
+        out_shape=(
+            jax.ShapeDtypeStruct((NPR, GR // 8, 2, 8, 128), F32),
+            jax.ShapeDtypeStruct((NPR, 1, PLACES), jnp.int32),
+        ),
+        in_specs=[pl.BlockSpec(memory_space=pltpu.SMEM)] + [vmem] * 5,
+        out_specs=(vmem, vmem),
+        scratch_shapes=[
+            pltpu.VMEM((GR // 8, 2, 8, 128), F32),
+            pltpu.VMEM((NPR * NPC, QR, 128), F32),
+            pltpu.VMEM((NPR * NPC, QR, 128), F32),
+            pltpu.VMEM((CH, CH), BF16),
+            pltpu.VMEM((CH, CH), BF16),
+            dma((NPR * NPC,)),
+            dma((NPR * NPC,)),
+            dma((NPR,)),
+            dma((NPR,)),
+        ],
+        compiler_params=pltpu.CompilerParams(
+            collective_id=1, has_side_effects=True, vmem_limit_bytes=VMEM_LIMIT
+        ),
+        name="exchange",
+    )(order, col_targets.reshape(CH, 1), col_targets.reshape(1, CH), col_all.reshape(16, 128), places, x)
+
+
+OUT_ROWS = 512
+PLACES = 384
+
+
+def place_kernel(place, weights, kaula, rows, goce, out, moved):
+    step = pl.program_id(0)
+    row_id, col_id = lax.axis_index("prow"), lax.axis_index("pcol")
+
+    @pl.when(step < NPR)
+    def _():
+        base = step * PLACES
 
         def scatter(i, carry):
-            for u in range(8):
-                moved[pl.ds(place[base + i * 8 + u], 1), :] = rows[i, u : u + 1, :]
+            for u in range(16):
+                at = place[base + i * 16 + u]
+                tile, sub = i * 2 + u // 8, u % 8
+                moved[pl.ds(at, 1), :] = rows[0, tile, 0, sub : sub + 1, :]
+                moved[pl.ds(at + 8, 1), :] = rows[0, tile, 1, sub : sub + 1, :]
             return carry
 
-        lax.fori_loop(0, GR // 8, scatter, 0)
+        lax.fori_loop(0, GR // 16, scatter, 0)
 
     @pl.when(step >= NPR)
     def _():
-        part = step - NPR
-        first = pl.multiple_of(part * OUT_ROWS, OUT_ROWS)
-        out[...] = weights[0] * moved[pl.ds(first, OUT_ROWS), :] + weights[1] * goce[...]
+        first = pl.multiple_of((step - NPR) * 2 * OUT_ROWS, OUT_ROWS)
+        block = moved[pl.ds(first, 2 * OUT_ROWS), :].reshape(OUT_ROWS // 8, 2, 8, 128)
+        for h in range(2):
+            cols = slice(h * 128, h * 128 + 128)
+            out[:, cols] = weights[0] * block[:, h].reshape(OUT_ROWS, 128) + weights[1] * goce[:, cols]
 
     @pl.when((step == NPR) & (row_id % NPC == col_id))
     def _():
@@ -141,29 +257,26 @@
             out[:BLOCK, cols] = out[:BLOCK, cols] + add
 
 
-def unpack(place, weights, col_all, kaula, received, goce):
+def place_rows(place, weights, kaula, rows, goce):
     return pl.pallas_call(
-        unpack_kernel,
+        place_kernel,
         out_shape=jax.ShapeDtypeStruct((RH, CH), F32),
         grid_spec=pltpu.PrefetchScalarGridSpec(
             num_scalar_prefetch=2,
             grid=(NPR + RH // OUT_ROWS,),
             in_specs=[
-                pl.BlockSpec((16, 128), lambda i, *_: (0, 0)),
                 pl.BlockSpec((1, CH), lambda i, *_: (0, 0)),
-                pl.BlockSpec((NPC, QR, 128), lambda i, *_: (jnp.minimum(i, NPR - 1), 0, 0)),
+                pl.BlockSpec(
+                    (1, GR // 8, 2, 8, 128), lambda i, *_: (jnp.minimum(i, NPR - 1), 0, 0, 0, 0)
+                ),
                 pl.BlockSpec((OUT_ROWS, CH), lambda i, *_: (jnp.maximum(i - NPR, 0), 0)),
             ],
             out_specs=pl.BlockSpec((OUT_ROWS, CH), lambda i, *_: (jnp.maximum(i - NPR, 0), 0)),
-            scratch_shapes=[
-                pltpu.VMEM((RH, CH), F32),
-                pltpu.VMEM((GR // 8, 8, CH), F32),
-                pltpu.VMEM((CH, CH), BF16),
-            ],
+            scratch_shapes=[pltpu.VMEM((2 * RH, 128), F32)],
         ),
         compiler_params=pltpu.CompilerParams(vmem_limit_bytes=VMEM_LIMIT),
-        name="unpack",
-    )(place, weights, col_all.reshape(16, 128), kaula.reshape(1, CH), received, goce)
+        name="place_rows",
+    )(place, weights, kaula.reshape(1, CH), rows, goce)
 
 
 def eliminate(group, carry, factor_t, inverse):
@@ -490,13 +603,13 @@
     row_id, col_id = lax.axis_index("prow"), lax.axis_index("pcol")
     targets = lax.dynamic_slice_in_dim(row_target, row_id * RH, RH)
     targets, order = lax.sort((targets, jnp.arange(RH, dtype=jnp.int32)), num_keys=1)
-    place = lax.all_to_all(targets.reshape(NPR, GR), "prow", split_axis=0, concat_axis=0, tiled=True)
-    place = place.reshape(RH) - row_id * RH
+    local = targets.reshape(NPR, 1, GR) - jnp.arange(NPR, dtype=jnp.int32)[:, None, None] * RH
+    places = jnp.pad(linear(local), ((0, 0), (0, 0), (0, PLACES - GR)))
     col_targets = lax.dynamic_slice_in_dim(column_target, col_id * CH, CH)
-    packed = pack(order, col_targets, grace_slab)
-    received = lax.all_to_all(packed, ("prow", "pcol"), split_axis=0, concat_axis=0, tiled=True)
+    split_rows = grace_slab.reshape(RH // 8, 8, 2, 128).transpose(0, 2, 1, 3).reshape(2 * RH, 128)
+    rows, places = exchange(linear(order), col_targets, column_target, places, split_rows)
     weights = jnp.concatenate([grace_weight, goce_weight])
-    combined = unpack(place, weights, column_target, kaula_prior, received, goce_slab)
+    combined = place_rows(places.reshape(-1), weights, kaula_prior, rows, goce_slab)
     return panel_step(combined)
 
 

time: 336 us -> 315 us (0.938)
  waiting for transfers between devices: 65.2 us -> 0 us
  Pallas kernels: 235 us -> 297 us
  starting transfers between devices: 16.7 us -> 0 us
    all_to_all x2 -> x0, waiting for transfers between devices: 65.2 us -> none  [the longest x1 65.2 us: shards(): lax.all_to_all(packed, ('prow', 'pcol'), split_axis=0, concat_axis=0, til...]
    pallas_call x2, Pallas kernels: 65.1 us -> 125 us  [the longest x1 103 us: exchange(): pl.pallas_call(exchange_kernel, out_shape=(jax.ShapeDtypeStruct((NPR, GR...]
    all_to_all x2 -> x0, starting transfers between devices: 16.7 us -> none  [the longest x1 9.69 us: shards(): lax.all_to_all(packed, ('prow', 'pcol'), split_axis=0, concat_axis=0, til...]
  transfers between devices with their start and end apart: 2 -> 0, of which waited for: 1 -> 0; matrix products, arithmetic and copies ran while one was open for 1% -> 0% of each run, Pallas kernels for 9% -> 0%
where the time goes in v2:
time: 315 us; the launch traced here: 314 us
  Pallas kernels  297 us (94%)
  local copies, waits for them, and re-layouts  8.64 us (3%)
  other arithmetic  7.62 us (2%)
    pallas_call x1, Pallas kernels, panel_step(): pl.pallas_call(panel_kernel, out_shape=jax.ShapeDtypeStruct((RH, CH), F32...  172 us
    pallas_call x1, Pallas kernels, exchange(): pl.pallas_call(exchange_kernel, out_shape=(jax.ShapeDtypeStruct((NPR, GR...  103 us
    pallas_call x1, Pallas kernels, place_rows(): pl.pallas_call(place_kernel, out_shape=jax.ShapeDtypeStruct((RH, CH), F32...  22.1 us

profile of v2, /device:TPU:7, one launch (start us, length us, event | category | flops | bytes accessed | tf_op | source)
XLA Modules:
  0.0 314.3 jit_solution(2805134149911557907)
XLA Ops:
  1.3 0.6 pad_maximum_fusion.weights
  1.9 0.8 dynamic_slice.7
  2.6 0.0 copy-start
  2.6 0.8 dynamic_slice.6
  3.5 6.2 %sort.15 = (s32[5632]{0:T(1024)S(1)}, s32[5632]{0:T(1024)S(1)}) sort(s32[5632]{0:T(1024)S(1)} %dynamic_slice.6, s32[5632]{0:T(1024)S(1)} %iota.8), dimensions={0}, to_apply=%region_0.0 | sort | flops 73216 | bytes 90112 | tf_op jit(solution)/shard_map/sort | solution.py:605
  9.6 0.6 fusion.2.order
  10.3 0.1 reshape.161
  10.4 0.3 fusion
  10.6 0.6 pad.4.places
  11.2 0.8 copy.8.col_down
  12.0 0.0 copy-done
  12.0 102.7 %exchange.1 = (f32[16,44,2,8,128]{4,3,2,1,0:T(8,128)}, s32[16,1,384]{2,1,0:T(1,128)}) custom-call(s32[5632]{0:T(1024)} %fusion.2.order, s32[256,1]{1,0:T(8,128)} %copy.8.col_down, s32[1,256]{1,0:T(1,128)} %bitcast.14, s32[16,128]{1,0:T(8,128)} %bitcast.12, s32[16,1,384]{2,1,0:T(1,128)} %pad.4.places, f32[11264,128]{1,0:T(8,128)} %bitcast.10), custom_call_target="tpu_custom_call" | custom-call | tf_op jit(solution)/shard_map/exchange/pallas_call | solution.py:195
  114.8 22.1 %place_rows.1.a_hbm = f32[5632,256]{1,0:T(8,128)} custom-call(s32[6144]{0:T(1024)} %bitcast.11, f32[2]{0:T(128)} %pad_maximum_fusion.weights, f32[1,256]{1,0:T(1,128)} %bitcast.15, f32[16,44,2,8,128]{4,3,2,1,0:T(8,128)} %get-tuple-element.12.rows, f32[5632,256]{1,0:T(8,128)} %goce.1), custom_call_target="tpu_custom_call" | custom-call | tf_op jit(solution)/shard_map/place_rows/pallas_call | solution.py:261
  136.9 171.8 %panel_step.1 = f32[5632,256]{1,0:T(8,128)} custom-call(f32[5632,256]{1,0:T(8,128)} %place_rows.1.a_hbm), custom_call_target="tpu_custom_call" | custom-call | tf_op jit(solution)/shard_map/panel_step/pallas_call | solution.py:570
  308.7 5.5 %copy.12 = f32[5632,256]{1,0:T(8,128)} copy(f32[5632,256]{1,0:T(8,128)} %panel_step.1) | data formatting | bytes 11534336
  (2 shorter events, 0.0 us)
Async XLA Ops:
  2.6 9.4 %copy-start = (s32[256]{0:T(256)}, s32[256]{0:T(256)S(1)}, u32[]{:S(2)}) copy-start(s32[256]{0:T(256)S(1)} %dynamic_slice.7) | copy-start | bytes 3076

commit v3 on v2

v3 whole, which is shorter than its diff:
```python
import functools

import jax
import jax.numpy as jnp
from jax import lax
from jax.experimental import pallas as pl
from jax.experimental.pallas import tpu as pltpu
from jax.sharding import PartitionSpec as P

F32, BF16 = jnp.float32, jnp.bfloat16
MESH = pl.DeviceIdType.MESH
HIGHEST = lax.Precision.HIGHEST
PANEL, BLOCK = 512, 128
NPR, NPC = 16, 8
RH, CH = 5632, 256
GR, GC = RH // NPR, CH // NPC
QR = GR // 4
PIECES = [(0, BLOCK)] + [(at, 256) for at in range(BLOCK, RH - 256, 256)] + [(RH - BLOCK, BLOCK)]
NC = len(PIECES)
VMEM_LIMIT = 60 * 2**20


def iota(shape, dim):
    return lax.broadcasted_iota(jnp.int32, shape, dim)


def select_columns(values, onehot):
    high = values.astype(BF16)
    rest = values - high.astype(F32)
    middle = rest.astype(BF16)
    low = (rest - middle.astype(F32)).astype(BF16)
    dot = functools.partial(jnp.dot, preferred_element_type=F32)
    return dot(high, onehot) + dot(middle, onehot) + dot(low, onehot)


def regroup(parts, lane):
    results = []
    for m in range(4):
        joined = None
        for k in range(4):
            moved = parts[k] if k == m else pltpu.roll(parts[k], ((k - m) * GC) % 128, 1)
            joined = moved if k == 0 else jnp.where(lane // GC == k, moved, joined)
        results.append(joined)
    return results


def linear(row):
    return row // 8 * 16 + row % 8


def turn_row(row_id, col_id, step):
    return jnp.bitwise_xor(row_id, lax.rem(step + 2 * col_id, NPR))


def turn_col(row_id, col_id, k):
    return jnp.bitwise_xor(col_id, lax.rem(k + row_id, NPC))


def exchange_kernel(
    order, col_all, places, x, out, places_out,
    rows, packed, received, pick_out, pick_in, sent, got, place_sent, place_got,
):
    row_id, col_id = lax.axis_index("prow"), lax.axis_index("pcol")
    me = row_id * NPC + col_id
    lane = iota((QR, 128), 1)

    barrier = pltpu.get_barrier_semaphore()

    def greet(k, carry):
        to = lax.rem(me + k, NPR * NPC)
        pl.semaphore_signal(barrier, inc=1, device_id=(to // NPC, to % NPC), device_id_type=MESH)
        return carry

    lax.fori_loop(1, NPR * NPC, greet, 0)

    mine = [col_all[pl.ds(col_id * 2 + h, 1), :].astype(F32) for h in range(2)]
    across = jnp.concatenate(mine, axis=1)
    down = jnp.concatenate([jnp.transpose(jnp.broadcast_to(v, (128, 128))) for v in mine], axis=0)
    below = (jnp.concatenate([down, down], axis=1) > across).astype(F32)
    rank = jnp.sum(below, axis=1, keepdims=True).astype(jnp.int32)
    pick_out[...] = jnp.where(rank == iota((CH, CH), 1), 1.0, 0.0).astype(BF16)

    def pack(step):
        dest = turn_row(row_id, col_id, step)
        base = dest * GR

        def gather(i, carry):
            for u in range(16):
                at = order[base + i * 16 + u]
                tile, sub = i * 2 + u // 8, u % 8
                rows[tile, 0, sub : sub + 1, :] = x[pl.ds(at, 1), :]
                rows[tile, 1, sub : sub + 1, :] = x[pl.ds(at + 8, 1), :]
            return carry

        lax.fori_loop(0, GR // 16, gather, 0)
        taken = jnp.concatenate([rows[:, h].reshape(GR, 128) for h in range(2)], axis=1)
        picked = select_columns(taken, pick_out[...])
        for half in range(2):
            parts = [picked[g * QR : (g + 1) * QR, half * 128 : half * 128 + 128] for g in range(4)]
            for q, joined in enumerate(regroup(parts, lane)):
                packed[dest * NPC + half * 4 + q] = joined

    def chunk_copy(row, col):
        other = row * NPC + col
        return pltpu.make_async_remote_copy(
            packed.at[other], received.at[me], sent.at[other], got.at[me],
            device_id=(row, col), device_id_type=MESH,
        )

    def chunk_from(row, col):
        other = row * NPC + col
        return pltpu.make_async_remote_copy(
            packed.at[other], received.at[other], sent.at[other], got.at[other],
            device_id=(row, col), device_id_type=MESH,
        )

    def place_copy(row, slot):
        return pltpu.make_async_remote_copy(
            places.at[row], places_out.at[slot], place_sent.at[row], place_got.at[slot],
            device_id=(row, col_id), device_id_type=MESH,
        )

    def own_copy():
        return pltpu.make_async_copy(packed.at[me], received.at[me], got.at[me])

    def own_places():
        return pltpu.make_async_copy(places.at[row_id], places_out.at[row_id], place_got.at[row_id])

    def each(step, remote, local):
        row = turn_row(row_id, col_id, step)
        for k in range(NPC):
            col = turn_col(row_id, col_id, k)
            inside = (row == row_id) & (col == col_id)

            @pl.when(jnp.logical_not(inside))
            def _(col=col):
                remote(row, col)

            if local is not None:
                pl.when(inside)(local)

    pack(0)
    pl.semaphore_wait(barrier, NPR * NPC - 1)

    def forward(step, carry):
        @pl.when(step < NPR - 1)
        def _():
            pack(step + 1)

        row = turn_row(row_id, col_id, step)

        @pl.when(row != row_id)
        def _():
            place_copy(row, row_id).start()

        @pl.when(row == row_id)
        def _():
            own_places().start()

        each(step, lambda r, c: chunk_copy(r, c).start(), lambda: own_copy().start())
        return carry

    lax.fori_loop(0, NPR, forward, 0)

    source = jnp.zeros((CH, 128), F32)
    here = col_id * CH + iota((CH, 128), 0)
    for r in range(16):
        source += jnp.where(col_all[r : r + 1, :] == here, float(r // 2), 0.0)
    source = jnp.sum(source, axis=1, keepdims=True)
    across = jnp.transpose(jnp.broadcast_to(source, (CH, 128)))[0:1, :]
    earlier = (source == across) & (iota((CH, CH), 0) < iota((CH, CH), 1))
    rank = jnp.sum(jnp.where(earlier, 1.0, 0.0), axis=0, keepdims=True)
    arrival = (across * GC + rank).astype(jnp.int32)
    pick_in[...] = jnp.where(iota((CH, CH), 0) == arrival, 1.0, 0.0).astype(BF16)

    def arrive(step, carry):
        origin = turn_row(row_id, col_id, step)

        @pl.when(origin != row_id)
        def _():
            place_copy(origin, origin).wait_recv()

        @pl.when(origin == row_id)
        def _():
            own_places().wait()

        each(step, lambda r, c: chunk_from(r, c).wait_recv(), lambda: own_copy().wait())
        halves = [regroup([received[origin * NPC + h * 4 + q] for q in range(4)], lane) for h in range(2)]
        joined = jnp.concatenate(
            [jnp.concatenate([halves[0][g], halves[1][g]], axis=1) for g in range(4)], axis=0
        )
        picked = select_columns(joined, pick_in[...])
        for h in range(2):
            out[origin, :, h] = picked[:, h * 128 : h * 128 + 128].reshape(GR // 8, 8, 128)
        return carry

    lax.fori_loop(0, NPR, arrive, 0)

    def leave(step, carry):
        row = turn_row(row_id, col_id, step)

        @pl.when(row != row_id)
        def _():
            place_copy(row, row_id).wait_send()

        each(step, lambda r, c: chunk_copy(r, c).wait_send(), None)
        return carry

    lax.fori_loop(0, NPR, leave, 0)


def exchange(order, col_all, places, x):
    dma, vmem = pltpu.SemaphoreType.DMA, pl.BlockSpec(memory_space=pltpu.VMEM)
    return pl.pallas_call(
        exchange_kernel,
        out_shape=(
            jax.ShapeDtypeStruct((NPR, GR // 8, 2, 8, 128), F32),
            jax.ShapeDtypeStruct((NPR, 1, GR), jnp.int32),
        ),
        in_specs=[pl.BlockSpec(memory_space=pltpu.SMEM)] + [vmem] * 3,
        out_specs=(vmem, vmem),
        scratch_shapes=[
            pltpu.VMEM((GR // 8, 2, 8, 128), F32),
            pltpu.VMEM((NPR * NPC, QR, 128), F32),
            pltpu.VMEM((NPR * NPC, QR, 128), F32),
            pltpu.VMEM((CH, CH), BF16),
            pltpu.VMEM((CH, CH), BF16),
            dma((NPR * NPC,)),
            dma((NPR * NPC,)),
            dma((NPR,)),
            dma((NPR,)),
        ],
        compiler_params=pltpu.CompilerParams(
            collective_id=1, has_side_effects=True, vmem_limit_bytes=VMEM_LIMIT
        ),
        name="exchange",
    )(order, col_all.reshape(16, 128), places, x)


STEPS = 4
STEP_PARTS, OUT_ROWS = NPR // STEPS, RH // STEPS


def place_kernel(place, weight_a, weight_b, kaula, rows, goce, out, moved):
    step = pl.program_id(0)
    row_id, col_id = lax.axis_index("prow"), lax.axis_index("pcol")

    @pl.when(step < STEPS)
    def _():
        for part in range(STEP_PARTS):
            source = step * STEP_PARTS + part

            def scatter(i, carry, part=part, source=source):
                for u in range(16):
                    at = place[source, 0, i * 16 + u]
                    tile, sub = i * 2 + u // 8, u % 8
                    moved[pl.ds(at, 1), :] = rows[part, tile, 0, sub : sub + 1, :]
                    moved[pl.ds(at + 8, 1), :] = rows[part, tile, 1, sub : sub + 1, :]
                return carry

            lax.fori_loop(0, GR // 16, scatter, 0)

    @pl.when(step >= STEPS)
    def _():
        first = pl.multiple_of((step - STEPS) * 2 * OUT_ROWS, 2 * OUT_ROWS)
        block = moved[pl.ds(first, 2 * OUT_ROWS), :].reshape(OUT_ROWS // 8, 2, 8, 128)
        for h in range(2):
            cols = slice(h * 128, h * 128 + 128)
            out[:, cols] = weight_a[0] * block[:, h].reshape(OUT_ROWS, 128) + weight_b[0] * goce[:, cols]

    @pl.when((step == STEPS) & (row_id % NPC == col_id))
    def _():
        equal = iota((BLOCK, BLOCK), 0) == iota((BLOCK, BLOCK), 1)
        for half in range(2):
            cols = slice(half * BLOCK, (half + 1) * BLOCK)
            add = jnp.where(equal & (row_id // NPC == half), kaula[:, cols], 0.0)
            out[:BLOCK, cols] = out[:BLOCK, cols] + add


def place_rows(place, weight_a, weight_b, kaula, rows, goce):
    smem = pl.BlockSpec(memory_space=pltpu.SMEM)
    return pl.pallas_call(
        place_kernel,
        out_shape=jax.ShapeDtypeStruct((RH, CH), F32),
        grid=(2 * STEPS,),
        in_specs=[
            smem,
            smem,
            smem,
            pl.BlockSpec((1, CH), lambda i: (0, 0)),
            pl.BlockSpec(
                (STEP_PARTS, GR // 8, 2, 8, 128), lambda i: (jnp.minimum(i, STEPS - 1), 0, 0, 0, 0)
            ),
            pl.BlockSpec((OUT_ROWS, CH), lambda i: (jnp.maximum(i - STEPS, 0), 0)),
        ],
        out_specs=pl.BlockSpec((OUT_ROWS, CH), lambda i: (jnp.maximum(i - STEPS, 0), 0)),
        scratch_shapes=[pltpu.VMEM((2 * RH, 128), F32)],
        compiler_params=pltpu.CompilerParams(vmem_limit_bytes=VMEM_LIMIT),
        name="place_rows",
    )(place, weight_a, weight_b, kaula.reshape(1, CH), rows, goce)


def across_rows(v, s):
    return jnp.broadcast_to(v[s : s + 1, :], (8, 128))


def across_lanes(v, t):
    return jnp.broadcast_to(v[:, t : t + 1], (8, 128))


def eliminate(group, carry, n, factor_t, inverse):
    d, x = list(carry[:n]), list(carry[n:])
    lane, sub = iota((8, 128), 1), iota((8, 128), 0)
    f_rows, x_rows = jnp.zeros((8, 128), F32), jnp.zeros((8, 128), F32)
    pivots = jnp.ones((8, 128), F32)
    z, zx = d[0], x[0]
    own = [across_lanes(z, t) for t in range(8)]
    for s in range(8):
        here = sub == s
        pivot, row, x_row = across_rows(own[s], s), across_rows(z, s), across_rows(zx, s)
        r = pltpu.reciprocal(pivot, approx=True)
        r = r * (2.0 - pivot * r)
        r = r * (2.0 - pivot * r)
        f_rows, x_rows = jnp.where(here, row, f_rows), jnp.where(here, x_row, x_rows)
        pivots = jnp.where(here, pivot, pivots)
        c = own[s] * r
        z = jnp.where(here, row * r, z - c * row)
        zx = jnp.where(here, x_row * r, zx - c * x_row)
        for t in range(s + 1, 8):
            e = across_rows(own[t], s)
            own[t] = jnp.where(here, e * r, own[t] - c * e)
    q = lax.rsqrt(pivots)
    q = q * (1.5 - 0.5 * pivots * q * q)
    at = pl.ds(pl.multiple_of(group * 8, 8), 8)
    live = (lane < 128 - 8 * group) & (lane >= sub)
    factor_t[at, :] = pltpu.roll(jnp.where(live, f_rows * q, 0.0), group * 8, 1)
    inverse[at, :] = x_rows * q
    z_rows, zx_rows = [across_rows(z, t) for t in range(8)], [across_rows(zx, t) for t in range(8)]
    for i in range(1, n):
        di, xi = d[i], x[i]
        for t in range(8):
            c = across_lanes(d[i], t)
            di = di - c * z_rows[t]
            xi = xi - c * zx_rows[t]
        d[i], x[i] = di, xi
    return tuple([pltpu.roll(v, 120, 1) for v in d[1:] + d[:1]] + x[1:] + x[:1])


def panel_kernel(
    a_hbm, out, a, panel, heads, work, factor_t, w_high, w_low, diag_f, diag_x,
    load, sent0, got0, sent1, got1, sent2, got2, head_sent, head_got,
):
    row_id, col_id = lax.axis_index("prow"), lax.axis_index("pcol")
    cx, cy = col_id // 2, col_id % 2
    cz, cyc = row_id // 4, row_id % 4
    left = cx < 2
    b = jnp.where(left, cx, 3 - cx)
    own = b * 2 + cy
    cross = (row_id, (3 - cx) * 2 + cy)
    x_mate = (row_id, (cx + 1 - 2 * (cx % 2)) * 2 + cy)
    y_mate = (row_id, cx * 2 + 1 - cy)
    over_z = [(lax.rem(cz + k, 4) * 4 + cyc, col_id) for k in (1, 2, 3)]
    core = cyc % 2
    y_near = (cz * 4 + lax.rem(cyc + 2, 4), col_id)
    core_mate = (cz * 4 + cyc + 1 - 2 * core, col_id)

    @pl.when(left)
    def _():
        pltpu.make_async_copy(a_hbm.at[:, pl.ds(0, BLOCK)], panel.at[own], load.at[0]).start()

    pltpu.make_async_copy(a_hbm, a, load.at[1]).start()
    barrier = pltpu.get_barrier_semaphore()
    for device in [cross, x_mate, y_mate, y_near, core_mate] + over_z:
        pl.semaphore_signal(barrier, inc=1, device_id=device, device_id_type=MESH)
    pl.semaphore_wait(barrier, 8)

    @pl.when(left)
    def _():
        pltpu.make_async_copy(a_hbm.at[:, pl.ds(0, BLOCK)], panel.at[own], load.at[0]).wait()

    def piece(j, c):
        return panel.at[j, pl.ds(*PIECES[c]), :]

    def send(j, c, sent, got, device):
        return pltpu.make_async_remote_copy(
            piece(j, c), piece(j, c), sent, got, device_id=device, device_id_type=MESH
        )

    flip_x, flip_y = (1 - b) * 2 + cy, b * 2 + 1 - cy
    flip_both = (1 - b) * 2 + 1 - cy

    def plan(c):
        if c % 2 == 0:
            return x_mate, flip_x, y_mate, flip_y
        return y_mate, flip_y, x_mate, flip_x

    def start0(c):
        @pl.when(left)
        def _():
            send(own, c, sent0.at[c], got0.at[c], cross).start()

    def start1(c):
        @pl.when(jnp.logical_not(left))
        def _():
            send(own, c, sent0.at[c], got0.at[c], cross).wait_recv()

        send(own, c, sent1.at[c], got1.at[c], plan(c)[0]).start()

    def start2(c):
        mate1, j1, mate2, _ = plan(c)
        send(j1, c, sent1.at[c], got1.at[c], mate1).wait_recv()
        send(own, c, sent2.at[c, 0], got2.at[c, 0], mate2).start()
        send(j1, c, sent2.at[c, 1], got2.at[c, 1], mate2).start()

    def finish2(c):
        _, _, mate2, j2 = plan(c)
        send(j2, c, sent2.at[c, 0], got2.at[c, 0], mate2).wait_recv()
        send(flip_both, c, sent2.at[c, 1], got2.at[c, 1], mate2).wait_recv()

    head = panel.at[:, pl.ds(0, BLOCK), :]
    a_owner = cyc == col_id % 4
    a_core = core == col_id % 2
    first_z = col_id // 4
    far = lax.rem(cyc + 2, 4)

    def head_local(slot):
        return pltpu.make_async_copy(head, heads.at[slot], head_got.at[slot])

    def head_copy(source, slot, k, device):
        return pltpu.make_async_remote_copy(
            source, heads.at[slot], head_sent.at[k], head_got.at[slot],
            device_id=device, device_id_type=MESH,
        )

    sources = [(cz == 0, cyc, 0), (a_owner & (cz == first_z), 4, 3), (a_owner & (cz == first_z + 2), 5, 6)]

    def head_z():
        for mine, slot, base in sources:

            @pl.when(mine)
            def _(slot=slot, base=base):
                head_local(slot).start()
                for k in range(3):
                    head_copy(head, slot, base + k, over_z[k]).start()

    def to_y(slot, k):
        return head_copy(heads.at[slot], slot, k, y_near)

    def to_core(slot, k):
        return head_copy(heads.at[slot], slot, k, core_mate)

    def head_y():
        head_local(cyc).wait()
        to_y(cyc, 9).start()

        @pl.when(a_owner)
        def _():
            for k, slot in enumerate((4, 5)):
                head_local(slot).wait()
                to_y(slot, 10 + k).start()

    def head_core():
        head_local(far).wait()
        to_core(cyc, 12).start()
        to_core(far, 13).start()

        @pl.when(a_core)
        def _():
            for k, slot in enumerate((4, 5)):

                @pl.when(jnp.logical_not(a_owner))
                def _(slot=slot):
                    head_local(slot).wait()

                to_core(slot, 14 + k).start()

    def head_in():
        head_local(cyc + 1 - 2 * core).wait()
        head_local(lax.rem(cyc + 3 - 2 * core, 4)).wait()

        @pl.when(jnp.logical_not(a_core))
        def _():
            for slot in (4, 5):
                head_local(slot).wait()

    def head_done():
        for mine, slot, base in sources:

            @pl.when(mine)
            def _(slot=slot, base=base):
                for k in range(3):
                    head_copy(head, slot, base + k, over_z[k]).wait_send()

        to_y(cyc, 9).wait_send()
        to_core(cyc, 12).wait_send()
        to_core(far, 13).wait_send()
        for k, slot in enumerate((4, 5)):

            @pl.when(a_owner)
            def _(k=k, slot=slot):
                to_y(slot, 10 + k).wait_send()

            @pl.when(a_core)
            def _(k=k, slot=slot):
                to_core(slot, 14 + k).wait_send()

    next0, next1, next2 = 6, 3, 2

    def advance():
        nonlocal next0, next1, next2
        if next0 < NC:
            start0(next0)
        if next1 < NC:
            start1(next1)
        if next2 < NC:
            start2(next2)
        next0, next1, next2 = next0 + 1, next1 + 1, next2 + 1

    for c in range(next0):
        start0(c)
    start1(0)
    start2(0)
    start1(1)
    finish2(0)
    head_z()
    start1(2)
    start2(1)
    advance()
    head_y()
    advance()
    head_core()
    advance()
    head_in()

    lower = iota((BLOCK, BLOCK), 0) >= iota((BLOCK, BLOCK), 1)
    for i in range(4):
        rows = slice(i * BLOCK, (i + 1) * BLOCK)
        for j in range(i):
            block = heads[i, j]
            work[rows, j * BLOCK : (j + 1) * BLOCK] = block
            work[j * BLOCK : (j + 1) * BLOCK, rows] = jnp.transpose(block)
        block = heads[i, i]
        work[rows, rows] = jnp.where(lower, block, jnp.transpose(block))
        for j in range(4):
            unit = jnp.where(iota((BLOCK, BLOCK), 0) == iota((BLOCK, BLOCK), 1), float(i == j), 0.0)
            work[rows, PANEL + j * BLOCK : PANEL + (j + 1) * BLOCK] = unit
            factor_t[rows, j * BLOCK : (j + 1) * BLOCK] = jnp.zeros((BLOCK, BLOCK), F32)

    for k in range(4):
        rows = slice(k * BLOCK, (k + 1) * BLOCK)
        carry = [work[k * BLOCK + g * 8 : k * BLOCK + g * 8 + 8, rows] for g in range(16)]
        carry += [
            work[k * BLOCK + g * 8 : k * BLOCK + g * 8 + 8, PANEL + k * BLOCK : PANEL + (k + 1) * BLOCK]
            for g in range(16)
        ]
        d, x = carry[:16], carry[16:]
        for part in range(4):
            n = 16 - 4 * part
            carry = lax.fori_loop(
                part * 4, part * 4 + 4, lambda g, v, n=n: eliminate(g, v, n, diag_f, diag_x), tuple(d + x)
            )
            d, x = list(carry[: n - 4]), list(carry[n : 2 * n - 4])
            if part in (0, 2):
                advance()
        factor_t[rows, rows] = diag_f[...]
        right = (k + 1) * BLOCK
        width = PANEL + (k + 1) * BLOCK - right
        solved = jnp.dot(diag_x[...], work[rows, right : right + width], precision=HIGHEST)
        work[rows, right : right + width] = solved
        count = PANEL - right
        if count:
            factor_t[rows, right:PANEL] = solved[:, :count]
            turned = jnp.transpose(solved[:, :count])
            work[right:PANEL, right : right + width] -= jnp.dot(turned, solved, precision=HIGHEST)

    columns = jnp.concatenate(
        [jnp.concatenate([heads[4 + i, j] for j in range(4)], axis=1) for i in range(2)], axis=0
    )
    solved = lax.dot_general(
        work[:, PANEL:], columns, (((1,), (1,)), ((), ())), precision=HIGHEST, preferred_element_type=F32
    )
    turned = jnp.transpose(work[:, PANEL:])
    weight = jnp.dot(turned, solved, precision=HIGHEST)
    work[:, :PANEL] = turned
    own_panel = col_id < PANEL // BLOCK
    direct = -work[:, pl.ds(pl.multiple_of(jnp.minimum(col_id, 3) * BLOCK, BLOCK), BLOCK)]
    weight = jnp.concatenate([jnp.where(own_panel, direct, weight[:, :BLOCK]), weight[:, BLOCK:]], axis=1)
    high = weight.astype(BF16)
    w_high[...] = high
    w_low[...] = (weight - high.astype(F32)).astype(BF16)
    pltpu.make_async_copy(a_hbm, a, load.at[1]).wait()
    dot = functools.partial(jnp.dot, preferred_element_type=F32)

    def update(c):
        if c:
            finish2(c)
        start, size = PIECES[c]
        at = slice(start, start + size)
        in_panel = iota((size, CH), 1) < jnp.where(own_panel, BLOCK, 0)
        left_rows = jnp.concatenate([panel[j, at, :] for j in range(4)], axis=1)
        high = left_rows.astype(BF16)
        low = (left_rows - high.astype(F32)).astype(BF16)
        product = dot(high, w_high[...]) + (dot(high, w_low[...]) + dot(low, w_high[...]))
        out[at, :] = jnp.where(in_panel, 0.0, a[at, :]) - product
        if c == 0:

            @pl.when(row_id < PANEL // BLOCK)
            def _():
                d, j = jnp.minimum(row_id, 3), jnp.minimum(col_id, 3)
                block = factor_t[
                    pl.ds(pl.multiple_of(j * BLOCK, BLOCK), BLOCK), pl.ds(pl.multiple_of(d * BLOCK, BLOCK), BLOCK)
                ]
                out[:BLOCK, :BLOCK] = jnp.where(own_panel, jnp.transpose(block), a[:BLOCK, :BLOCK])
                out[:BLOCK, BLOCK:] = a[:BLOCK, BLOCK:]

    done = 0
    while next2 < NC:
        advance()
        for _ in range(2):
            if done <= next2 - 4:
                update(done)
                done += 1
    while done < NC:
        update(done)
        done += 1

    for c in range(NC):

        @pl.when(left)
        def _(c=c):
            send(own, c, sent0.at[c], got0.at[c], cross).wait_send()

        mate1, j1, mate2, _ = plan(c)
        send(own, c, sent1.at[c], got1.at[c], mate1).wait_send()
        send(own, c, sent2.at[c, 0], got2.at[c, 0], mate2).wait_send()
        send(j1, c, sent2.at[c, 1], got2.at[c, 1], mate2).wait_send()
    head_done()


def panel_step(combined):
    dma = pltpu.SemaphoreType.DMA
    return pl.pallas_call(
        panel_kernel,
        out_shape=jax.ShapeDtypeStruct((RH, CH), F32),
        in_specs=[pl.BlockSpec(memory_space=pl.ANY)],
        out_specs=pl.BlockSpec(memory_space=pltpu.VMEM),
        scratch_shapes=[
            pltpu.VMEM((RH, CH), F32),
            pltpu.VMEM((4, RH, BLOCK), F32),
            pltpu.VMEM((6, 4, BLOCK, BLOCK), F32),
            pltpu.VMEM((PANEL, 2 * PANEL), F32),
            pltpu.VMEM((PANEL, PANEL), F32),
            pltpu.VMEM((PANEL, CH), BF16),
            pltpu.VMEM((PANEL, CH), BF16),
            pltpu.VMEM((BLOCK, BLOCK), F32),
            pltpu.VMEM((BLOCK, BLOCK), F32),
            dma((2,)),
            dma((NC,)),
            dma((NC,)),
            dma((NC,)),
            dma((NC,)),
            dma((NC, 2)),
            dma((NC, 2)),
            dma((16,)),
            dma((6,)),
        ],
        compiler_params=pltpu.CompilerParams(
            collective_id=0, has_side_effects=True, vmem_limit_bytes=VMEM_LIMIT
        ),
        name="panel_step",
    )(combined)


def shards(grace_slab, goce_slab, grace_weight, goce_weight, kaula_prior, row_target, column_target):
    row_id = lax.axis_index("prow")
    targets = lax.dynamic_slice_in_dim(row_target, row_id * RH, RH)
    targets, order = lax.sort((targets, jnp.arange(RH, dtype=jnp.int32)), num_keys=1)
    places = linear(targets.reshape(NPR, 1, GR) - jnp.arange(NPR, dtype=jnp.int32)[:, None, None] * RH)
    split_rows = grace_slab.reshape(RH // 8, 8, 2, 128).transpose(0, 2, 1, 3).reshape(2 * RH, 128)
    rows, places = exchange(linear(order), column_target, places, split_rows)
    combined = place_rows(places, grace_weight, goce_weight, kaula_prior, rows, goce_slab)
    return panel_step(combined)


def solution(mesh):
    return jax.shard_map(
        shards,
        mesh=mesh,
        in_specs=(P("prow", "pcol"), P("prow", "pcol"), P(), P(), P("pcol"), P(), P()),
        out_specs=P("prow", "pcol"),
        check_vma=False,
    )
```

time: 315 us -> 259 us (0.82)
  Pallas kernels: 297 us -> 243 us
    pallas_call x1, Pallas kernels: 172 us -> 126 us  [panel_step(): pl.pallas_call(panel_kernel, out_shape=jax.ShapeDtypeStruct((RH, CH), F32...]
    pallas_call x1, Pallas kernels: 103 us -> 95.9 us  [exchange(): pl.pallas_call(exchange_kernel, out_shape=(jax.ShapeDtypeStruct((NPR, GR...]
where the time goes in v3:
time: 259 us
  Pallas kernels  243 us (94%)
  other arithmetic  7.65 us (3%)
  local copies, waits for them, and re-layouts  6.47 us (2%)
    pallas_call x1, Pallas kernels, panel_step(): pl.pallas_call(panel_kernel, out_shape=jax.ShapeDtypeStruct((RH, CH), F32...  126 us
    pallas_call x1, Pallas kernels, exchange(): pl.pallas_call(exchange_kernel, out_shape=(jax.ShapeDtypeStruct((NPR, GR...  95.9 us
    pallas_call x1, Pallas kernels, place_rows(): pl.pallas_call(place_kernel, out_shape=jax.ShapeDtypeStruct((RH, CH), F32...  21.9 us
    sort x1, other arithmetic, shards(): lax.sort((targets, jnp.arange(RH, dtype=jnp.int32)), num_keys=1)  6.16 us
    unnamed x1, local copies, waits for them, and re-layouts  5.54 us

profile of v3, /device:TPU:7, one launch (start us, length us, event | category | flops | bytes accessed | tf_op | source)
XLA Modules:
  0.0 258.9 jit_solution(8270795286681228566)
XLA Ops:
  1.3 0.8 dynamic_slice.3
  2.1 6.2 %sort.15 = (s32[5632]{0:T(1024)S(1)}, s32[5632]{0:T(1024)S(1)}) sort(s32[5632]{0:T(1024)S(1)} %dynamic_slice.3, s32[5632]{0:T(1024)S(1)} %iota.8), dimensions={0}, to_apply=%region_0.0 | sort | flops 73216 | bytes 90112 | tf_op jit(solution)/shard_map/sort | solution.py:677
  8.3 0.6 fusion.2.order
  8.9 0.1 reshape.150
  9.0 0.9 fusion.places
  9.9 95.9 %exchange.1 = (f32[16,44,2,8,128]{4,3,2,1,0:T(8,128)}, s32[16,1,352]{2,1,0:T(1,128)}) custom-call(s32[5632]{0:T(1024)} %fusion.2.order, s32[16,128]{1,0:T(8,128)} %bitcast.8, s32[16,1,352]{2,1,0:T(1,128)} %fusion.places, f32[11264,128]{1,0:T(8,128)} %bitcast.7), custom_call_target="tpu_custom_call" | custom-call | tf_op jit(solution)/shard_map/exchange/pallas_call | solution.py:214
  105.9 21.9 %place_rows.1.a_hbm = f32[5632,256]{1,0:T(8,128)} custom-call(s32[16,1,352]{2,1,0:T(1,128)} %get-tuple-element.11.place, f32[1]{0:T(128)S(6)} %copy.9.weight_a, f32[1]{0:T(128)S(6)} %copy.10.weight_b, f32[1,256]{1,0:T(1,128)} %bitcast.9, f32[16,44,2,8,128]{4,3,2,1,0:T(8,128)} %get-tuple-element.12.rows, f32[5632,256]{1,0:T(8,128)} %goce.1), custom_call_target="tpu_custom_call" | custom-call | tf_op jit(solution)/shard_map/place_rows/pallas_call | solution.py:282
  127.8 125.6 %panel_step.1 = f32[5632,256]{1,0:T(8,128)} custom-call(f32[5632,256]{1,0:T(8,128)} %place_rows.1.a_hbm), custom_call_target="tpu_custom_call" | custom-call | tf_op jit(solution)/shard_map/panel_step/pallas_call | solution.py:642
  253.4 5.5 %copy.11 = f32[5632,256]{1,0:T(8,128)} copy(f32[5632,256]{1,0:T(8,128)} %panel_step.1) | data formatting | bytes 11534336
  (2 shorter events, 0.0 us)

commit v4 on v3

--- a/solution.py
+++ b/solution.py
@@ -18,6 +18,7 @@
 PIECES = [(0, BLOCK)] + [(at, 256) for at in range(BLOCK, RH - 256, 256)] + [(RH - BLOCK, BLOCK)]
 NC = len(PIECES)
 VMEM_LIMIT = 60 * 2**20
+INV_ROWS = 48
 
 
 def iota(shape, dim):
@@ -57,8 +58,8 @@
 
 
 def exchange_kernel(
-    order, col_all, places, x, out, places_out,
-    rows, packed, received, pick_out, pick_in, sent, got, place_sent, place_got,
+    order, col_all, places, x, out, inverse_out,
+    rows, packed, received, places_in, pick_out, pick_in, sent, got, place_sent, place_got,
 ):
     row_id, col_id = lax.axis_index("prow"), lax.axis_index("pcol")
     me = row_id * NPC + col_id
@@ -116,7 +117,7 @@
 
     def place_copy(row, slot):
         return pltpu.make_async_remote_copy(
-            places.at[row], places_out.at[slot], place_sent.at[row], place_got.at[slot],
+            places.at[row], places_in.at[slot], place_sent.at[row], place_got.at[slot],
             device_id=(row, col_id), device_id_type=MESH,
         )
 
@@ -124,7 +125,7 @@
         return pltpu.make_async_copy(packed.at[me], received.at[me], got.at[me])
 
     def own_places():
-        return pltpu.make_async_copy(places.at[row_id], places_out.at[row_id], place_got.at[row_id])
+        return pltpu.make_async_copy(places.at[row_id], places_in.at[row_id], place_got.at[row_id])
 
     def each(step, remote, local):
         row = turn_row(row_id, col_id, step)
@@ -141,21 +142,18 @@
 
     pack(0)
     pl.semaphore_wait(barrier, NPR * NPC - 1)
+    own_places().start()
+
+    def announce(k, carry):
+        place_copy(jnp.bitwise_xor(row_id, k), row_id).start()
+        return carry
+
+    lax.fori_loop(1, NPR, announce, 0)
 
     def forward(step, carry):
         @pl.when(step < NPR - 1)
         def _():
             pack(step + 1)
-
-        row = turn_row(row_id, col_id, step)
-
-        @pl.when(row != row_id)
-        def _():
-            place_copy(row, row_id).start()
-
-        @pl.when(row == row_id)
-        def _():
-            own_places().start()
 
         each(step, lambda r, c: chunk_copy(r, c).start(), lambda: own_copy().start())
         return carry
@@ -173,17 +171,33 @@
     arrival = (across * GC + rank).astype(jnp.int32)
     pick_in[...] = jnp.where(iota((CH, CH), 0) == arrival, 1.0, 0.0).astype(BF16)
 
+    own_places().wait()
+
+    def places_arrive(k, carry):
+        origin = jnp.bitwise_xor(row_id, k)
+        place_copy(origin, origin).wait_recv()
+        return carry
+
+    lax.fori_loop(1, NPR, places_arrive, 0)
+
+    def invert(origin, total):
+        place = places_in[origin]
+        number = origin * GR + iota((1, GR), 1)
+        high, low = number // 64, number % 64
+        down = iota((INV_ROWS, GR), 0) == lax.shift_right_logical(place, 7)
+        across = jnp.where(iota((BLOCK, GR), 0) == jnp.bitwise_and(place, 127), 1.0, 0.0).astype(BF16)
+        for part, scale in ((high, 64.0), (low, 1.0)):
+            values = jnp.where(down, part.astype(F32), 0.0).astype(BF16)
+            total = total + scale * lax.dot_general(
+                values, across, (((1,), (1,)), ((), ())), preferred_element_type=F32
+            )
+        return total
+
+    number = lax.fori_loop(0, NPR, invert, jnp.zeros((INV_ROWS, BLOCK), F32)).astype(jnp.int32)
+    inverse_out[...] = number + lax.shift_right_logical(number, 3) * 8
+
     def arrive(step, carry):
         origin = turn_row(row_id, col_id, step)
-
-        @pl.when(origin != row_id)
-        def _():
-            place_copy(origin, origin).wait_recv()
-
-        @pl.when(origin == row_id)
-        def _():
-            own_places().wait()
-
         each(step, lambda r, c: chunk_from(r, c).wait_recv(), lambda: own_copy().wait())
         halves = [regroup([received[origin * NPC + h * 4 + q] for q in range(4)], lane) for h in range(2)]
         joined = jnp.concatenate(
@@ -197,16 +211,16 @@
     lax.fori_loop(0, NPR, arrive, 0)
 
     def leave(step, carry):
-        row = turn_row(row_id, col_id, step)
-
-        @pl.when(row != row_id)
-        def _():
-            place_copy(row, row_id).wait_send()
-
         each(step, lambda r, c: chunk_copy(r, c).wait_send(), None)
         return carry
 
     lax.fori_loop(0, NPR, leave, 0)
+
+    def announced(k, carry):
+        place_copy(jnp.bitwise_xor(row_id, k), row_id).wait_send()
+        return carry
+
+    lax.fori_loop(1, NPR, announced, 0)
 
 
 def exchange(order, col_all, places, x):
@@ -215,7 +229,7 @@
         exchange_kernel,
         out_shape=(
             jax.ShapeDtypeStruct((NPR, GR // 8, 2, 8, 128), F32),
-            jax.ShapeDtypeStruct((NPR, 1, GR), jnp.int32),
+            jax.ShapeDtypeStruct((INV_ROWS, BLOCK), jnp.int32),
         ),
         in_specs=[pl.BlockSpec(memory_space=pltpu.SMEM)] + [vmem] * 3,
         out_specs=(vmem, vmem),
@@ -223,6 +237,7 @@
             pltpu.VMEM((GR // 8, 2, 8, 128), F32),
             pltpu.VMEM((NPR * NPC, QR, 128), F32),
             pltpu.VMEM((NPR * NPC, QR, 128), F32),
+            pltpu.VMEM((NPR, 1, GR), jnp.int32),
             pltpu.VMEM((CH, CH), BF16),
             pltpu.VMEM((CH, CH), BF16),
             dma((NPR * NPC,)),
@@ -235,69 +250,6 @@
         ),
         name="exchange",
     )(order, col_all.reshape(16, 128), places, x)
-
-
-STEPS = 4
-STEP_PARTS, OUT_ROWS = NPR // STEPS, RH // STEPS
-
-
-def place_kernel(place, weight_a, weight_b, kaula, rows, goce, out, moved):
-    step = pl.program_id(0)
-    row_id, col_id = lax.axis_index("prow"), lax.axis_index("pcol")
-
-    @pl.when(step < STEPS)
-    def _():
-        for part in range(STEP_PARTS):
-            source = step * STEP_PARTS + part
-
-            def scatter(i, carry, part=part, source=source):
-                for u in range(16):
-                    at = place[source, 0, i * 16 + u]
-                    tile, sub = i * 2 + u // 8, u % 8
-                    moved[pl.ds(at, 1), :] = rows[part, tile, 0, sub : sub + 1, :]
-                    moved[pl.ds(at + 8, 1), :] = rows[part, tile, 1, sub : sub + 1, :]
-                return carry
-
-            lax.fori_loop(0, GR // 16, scatter, 0)
-
-    @pl.when(step >= STEPS)
-    def _():
-        first = pl.multiple_of((step - STEPS) * 2 * OUT_ROWS, 2 * OUT_ROWS)
-        block = moved[pl.ds(first, 2 * OUT_ROWS), :].reshape(OUT_ROWS // 8, 2, 8, 128)
-        for h in range(2):
-            cols = slice(h * 128, h * 128 + 128)
-            out[:, cols] = weight_a[0] * block[:, h].reshape(OUT_ROWS, 128) + weight_b[0] * goce[:, cols]
-
-    @pl.when((step == STEPS) & (row_id % NPC == col_id))
-    def _():
-        equal = iota((BLOCK, BLOCK), 0) == iota((BLOCK, BLOCK), 1)
-        for half in range(2):
-            cols = slice(half * BLOCK, (half + 1) * BLOCK)
-            add = jnp.where(equal & (row_id // NPC == half), kaula[:, cols], 0.0)
-            out[:BLOCK, cols] = out[:BLOCK, cols] + add
-
-
-def place_rows(place, weight_a, weight_b, kaula, rows, goce):
-    smem = pl.BlockSpec(memory_space=pltpu.SMEM)
-    return pl.pallas_call(
-        place_kernel,
-        out_shape=jax.ShapeDtypeStruct((RH, CH), F32),
-        grid=(2 * STEPS,),
-        in_specs=[
-            smem,
-            smem,
-            smem,
-            pl.BlockSpec((1, CH), lambda i: (0, 0)),
-            pl.BlockSpec(
-                (STEP_PARTS, GR // 8, 2, 8, 128), lambda i: (jnp.minimum(i, STEPS - 1), 0, 0, 0, 0)
-            ),
-            pl.BlockSpec((OUT_ROWS, CH), lambda i: (jnp.maximum(i - STEPS, 0), 0)),
-        ],
-        out_specs=pl.BlockSpec((OUT_ROWS, CH), lambda i: (jnp.maximum(i - STEPS, 0), 0)),
-        scratch_shapes=[pltpu.VMEM((2 * RH, 128), F32)],
-        compiler_params=pltpu.CompilerParams(vmem_limit_bytes=VMEM_LIMIT),
-        name="place_rows",
-    )(place, weight_a, weight_b, kaula.reshape(1, CH), rows, goce)
 
 
 def across_rows(v, s):
@@ -347,7 +299,8 @@
 
 
 def panel_kernel(
-    a_hbm, out, a, panel, heads, work, factor_t, w_high, w_low, diag_f, diag_x,
+    inverse, weight_a, weight_b, kaula, rows_hbm, goce_hbm, out,
+    source, goce, raw, a, panel, heads, work, factor_t, w_high, w_low, diag_f, diag_x,
     load, sent0, got0, sent1, got1, sent2, got2, head_sent, head_got,
 ):
     row_id, col_id = lax.axis_index("prow"), lax.axis_index("pcol")
@@ -364,19 +317,43 @@
     y_near = (cz * 4 + lax.rem(cyc + 2, 4), col_id)
     core_mate = (cz * 4 + cyc + 1 - 2 * core, col_id)
 
-    @pl.when(left)
-    def _():
-        pltpu.make_async_copy(a_hbm.at[:, pl.ds(0, BLOCK)], panel.at[own], load.at[0]).start()
-
-    pltpu.make_async_copy(a_hbm, a, load.at[1]).start()
+    fetch = [
+        pltpu.make_async_copy(rows_hbm, source, load.at[0]),
+        pltpu.make_async_copy(goce_hbm, goce, load.at[1]),
+    ]
+    for copy in fetch:
+        copy.start()
     barrier = pltpu.get_barrier_semaphore()
     for device in [cross, x_mate, y_mate, y_near, core_mate] + over_z:
         pl.semaphore_signal(barrier, inc=1, device_id=device, device_id_type=MESH)
-    pl.semaphore_wait(barrier, 8)
-
-    @pl.when(left)
-    def _():
-        pltpu.make_async_copy(a_hbm.at[:, pl.ds(0, BLOCK)], panel.at[own], load.at[0]).wait()
+
+    def build(c):
+        start, size = PIECES[c]
+
+        def gather(i, carry):
+            for u in range(16):
+                at = inverse[start // 128 + i // 8, i % 8 * 16 + u]
+                tile, sub = i * 2 + u // 8, u % 8
+                raw[tile, 0, sub : sub + 1, :] = source[pl.ds(at, 1), :]
+                raw[tile, 1, sub : sub + 1, :] = source[pl.ds(at + 8, 1), :]
+            return carry
+
+        lax.fori_loop(0, size // 16, gather, 0)
+        at = slice(start, start + size)
+        for h in range(2):
+            cols = slice(h * BLOCK, (h + 1) * BLOCK)
+            moved = raw[: size // 8, h].reshape(size, BLOCK)
+            block = weight_a[0] * moved + weight_b[0] * goce[at, cols]
+            if c == 0:
+                diagonal = iota((BLOCK, BLOCK), 0) == iota((BLOCK, BLOCK), 1)
+                here = (row_id % NPC == col_id) & (row_id // NPC == h)
+                block = block + jnp.where(diagonal & here, kaula[:, cols], 0.0)
+            a[h, at] = block
+            if h == 0:
+
+                @pl.when(left)
+                def _():
+                    panel[own, at] = block
 
     def piece(j, c):
         return panel.at[j, pl.ds(*PIECES[c]), :]
@@ -514,17 +491,33 @@
             start1(next1)
         if next2 < NC:
             start2(next2)
+        if next0 + 1 < NC:
+            build(next0 + 1)
         next0, next1, next2 = next0 + 1, next1 + 1, next2 + 1
 
-    for c in range(next0):
-        start0(c)
+    for copy in fetch:
+        copy.wait()
+    build(0)
+    pl.semaphore_wait(barrier, 8)
+    build(1)
+    start0(0)
+    build(2)
+    start0(1)
     start1(0)
+    build(3)
+    start0(2)
     start2(0)
+    build(4)
+    start0(3)
     start1(1)
     finish2(0)
     head_z()
+    build(5)
+    start0(4)
     start1(2)
     start2(1)
+    build(6)
+    start0(5)
     advance()
     head_y()
     advance()
@@ -588,7 +581,6 @@
     high = weight.astype(BF16)
     w_high[...] = high
     w_low[...] = (weight - high.astype(F32)).astype(BF16)
-    pltpu.make_async_copy(a_hbm, a, load.at[1]).wait()
     dot = functools.partial(jnp.dot, preferred_element_type=F32)
 
     def update(c):
@@ -596,12 +588,12 @@
             finish2(c)
         start, size = PIECES[c]
         at = slice(start, start + size)
-        in_panel = iota((size, CH), 1) < jnp.where(own_panel, BLOCK, 0)
         left_rows = jnp.concatenate([panel[j, at, :] for j in range(4)], axis=1)
         high = left_rows.astype(BF16)
         low = (left_rows - high.astype(F32)).astype(BF16)
         product = dot(high, w_high[...]) + (dot(high, w_low[...]) + dot(low, w_high[...]))
-        out[at, :] = jnp.where(in_panel, 0.0, a[at, :]) - product
+        out[at, :BLOCK] = jnp.where(own_panel, 0.0, a[0, at]) - product[:, :BLOCK]
+        out[at, BLOCK:] = a[1, at] - product[:, BLOCK:]
         if c == 0:
 
             @pl.when(row_id < PANEL // BLOCK)
@@ -610,8 +602,8 @@
                 block = factor_t[
                     pl.ds(pl.multiple_of(j * BLOCK, BLOCK), BLOCK), pl.ds(pl.multiple_of(d * BLOCK, BLOCK), BLOCK)
                 ]
-                out[:BLOCK, :BLOCK] = jnp.where(own_panel, jnp.transpose(block), a[:BLOCK, :BLOCK])
-                out[:BLOCK, BLOCK:] = a[:BLOCK, BLOCK:]
+                out[:BLOCK, :BLOCK] = jnp.where(own_panel, jnp.transpose(block), a[0, :BLOCK])
+                out[:BLOCK, BLOCK:] = a[1, :BLOCK]
 
     done = 0
     while next2 < NC:
@@ -637,15 +629,19 @@
     head_done()
 
 
-def panel_step(combined):
+def panel_step(inverse, weight_a, weight_b, kaula, rows, goce):
     dma = pltpu.SemaphoreType.DMA
+    smem, anywhere = pl.BlockSpec(memory_space=pltpu.SMEM), pl.BlockSpec(memory_space=pl.ANY)
     return pl.pallas_call(
         panel_kernel,
         out_shape=jax.ShapeDtypeStruct((RH, CH), F32),
-        in_specs=[pl.BlockSpec(memory_space=pl.ANY)],
+        in_specs=[smem] * 3 + [pl.BlockSpec(memory_space=pltpu.VMEM), anywhere, anywhere],
         out_specs=pl.BlockSpec(memory_space=pltpu.VMEM),
         scratch_shapes=[
+            pltpu.VMEM((2 * RH, 128), F32),
             pltpu.VMEM((RH, CH), F32),
+            pltpu.VMEM((32, 2, 8, 128), F32),
+            pltpu.VMEM((2, RH, BLOCK), F32),
             pltpu.VMEM((4, RH, BLOCK), F32),
             pltpu.VMEM((6, 4, BLOCK, BLOCK), F32),
             pltpu.VMEM((PANEL, 2 * PANEL), F32),
@@ -668,18 +664,17 @@
             collective_id=0, has_side_effects=True, vmem_limit_bytes=VMEM_LIMIT
         ),
         name="panel_step",
-    )(combined)
+    )(inverse, weight_a, weight_b, kaula.reshape(1, CH), rows, goce)
 
 
 def shards(grace_slab, goce_slab, grace_weight, goce_weight, kaula_prior, row_target, column_target):
     row_id = lax.axis_index("prow")
     targets = lax.dynamic_slice_in_dim(row_target, row_id * RH, RH)
     targets, order = lax.sort((targets, jnp.arange(RH, dtype=jnp.int32)), num_keys=1)
-    places = linear(targets.reshape(NPR, 1, GR) - jnp.arange(NPR, dtype=jnp.int32)[:, None, None] * RH)
+    places = targets.reshape(NPR, 1, GR) - jnp.arange(NPR, dtype=jnp.int32)[:, None, None] * RH
     split_rows = grace_slab.reshape(RH // 8, 8, 2, 128).transpose(0, 2, 1, 3).reshape(2 * RH, 128)
-    rows, places = exchange(linear(order), column_target, places, split_rows)
-    combined = place_rows(places, grace_weight, goce_weight, kaula_prior, rows, goce_slab)
-    return panel_step(combined)
+    rows, inverse = exchange(linear(order), column_target, places, split_rows)
+    return panel_step(inverse, grace_weight, goce_weight, kaula_prior, rows.reshape(2 * RH, 128), goce_slab)
 
 
 def solution(mesh):

time: 259 us -> 244 us (0.942); the launches traced: 259 us -> 241 us
  Pallas kernels: 243 us -> 226 us
    pallas_call x1 -> x0, Pallas kernels: 21.9 us -> none  [place_rows(): pl.pallas_call(place_kernel, out_shape=jax.ShapeDtypeStruct((RH, CH), F32...]
    pallas_call x1, Pallas kernels: 126 us -> 130 us  [panel_step(): pl.pallas_call(panel_kernel, out_shape=jax.ShapeDtypeStruct((RH, CH), F32...]
where the time goes in v4:
time: 244 us; the launch traced here: 241 us
  Pallas kernels  226 us (93%)
  other arithmetic  7.48 us (3%)
  local copies, waits for them, and re-layouts  6.47 us (3%)
    pallas_call x1, Pallas kernels, panel_step(): pl.pallas_call(panel_kernel, out_shape=jax.ShapeDtypeStruct((RH, CH), F32...  130 us
    pallas_call x1, Pallas kernels, exchange(): pl.pallas_call(exchange_kernel, out_shape=(jax.ShapeDtypeStruct((NPR, GR...  95.9 us
    sort x1, other arithmetic, shards(): lax.sort((targets, jnp.arange(RH, dtype=jnp.int32)), num_keys=1)  6.16 us
    unnamed x1, local copies, waits for them, and re-layouts  5.54 us

profile of v4, /device:TPU:7, one launch (start us, length us, event | category | flops | bytes accessed | tf_op | source)
XLA Modules:
  0.0 241.2 jit_solution(7500756846455364389)
XLA Ops:
  1.3 0.8 dynamic_slice.3
  2.1 6.2 %sort.15 = (s32[5632]{0:T(1024)S(1)}, s32[5632]{0:T(1024)S(1)}) sort(s32[5632]{0:T(1024)S(1)} %dynamic_slice.3, s32[5632]{0:T(1024)S(1)} %iota.8), dimensions={0}, to_apply=%region_0.0 | sort | flops 73216 | bytes 90112 | tf_op jit(solution)/shard_map/sort | solution.py:673
  8.3 0.6 fusion.1.order
  8.9 0.1 reshape.57
  9.0 0.7 broadcast_subtract_fusion.places
  9.7 95.9 %exchange.1 = (f32[16,44,2,8,128]{4,3,2,1,0:T(8,128)}, s32[48,128]{1,0:T(8,128)}) custom-call(s32[5632]{0:T(1024)} %fusion.1.order, s32[16,128]{1,0:T(8,128)} %bitcast.10, s32[16,1,352]{2,1,0:T(1,128)} %broadcast_subtract_fusion.places, f32[11264,128]{1,0:T(8,128)} %bitcast.9), custom_call_target="tpu_custom_call" | custom-call | tf_op jit(solution)/shard_map/exchange/pallas_call | solution.py:228
  105.7 130.0 %panel_step.1 = f32[5632,256]{1,0:T(8,128)} custom-call(s32[48,128]{1,0:T(8,128)} %get-tuple-element.11.inverse, f32[1]{0:T(128)S(6)} %copy.9.weight_a, f32[1]{0:T(128)S(6)} %copy.10.weight_b, f32[1,256]{1,0:T(1,128)} %bitcast.11, f32[11264,128]{1,0:T(8,128)} %bitcast.8, f32[5632,256]{1,0:T(8,128)} %goce_hbm.1), custom_call_target="tpu_custom_call" | custom-call | tf_op jit(solution)/shard_map/panel_step/pallas_call | solution.py:635
  235.7 5.5 %copy.11 = f32[5632,256]{1,0:T(8,128)} copy(f32[5632,256]{1,0:T(8,128)} %panel_step.1) | data formatting | bytes 11534336
  (2 shorter events, 0.0 us)

commit v5 on v4

--- a/solution.py
+++ b/solution.py
@@ -58,8 +58,8 @@
 
 
 def exchange_kernel(
-    order, col_all, places, x, out, inverse_out,
-    rows, packed, received, places_in, pick_out, pick_in, sent, got, place_sent, place_got,
+    order, col_all, places, x, out, inverse_out, pick_in,
+    rows, packed, received, places_in, pick_out, sent, got, place_sent, place_got,
 ):
     row_id, col_id = lax.axis_index("prow"), lax.axis_index("pcol")
     me = row_id * NPC + col_id
@@ -200,12 +200,9 @@
         origin = turn_row(row_id, col_id, step)
         each(step, lambda r, c: chunk_from(r, c).wait_recv(), lambda: own_copy().wait())
         halves = [regroup([received[origin * NPC + h * 4 + q] for q in range(4)], lane) for h in range(2)]
-        joined = jnp.concatenate(
-            [jnp.concatenate([halves[0][g], halves[1][g]], axis=1) for g in range(4)], axis=0
-        )
-        picked = select_columns(joined, pick_in[...])
+        joined = [jnp.concatenate(half, axis=0) for half in halves]
         for h in range(2):
-            out[origin, :, h] = picked[:, h * 128 : h * 128 + 128].reshape(GR // 8, 8, 128)
+            out[origin, :, h] = joined[h].reshape(GR // 8, 8, 128)
         return carry
 
     lax.fori_loop(0, NPR, arrive, 0)
@@ -230,15 +227,15 @@
         out_shape=(
             jax.ShapeDtypeStruct((NPR, GR // 8, 2, 8, 128), F32),
             jax.ShapeDtypeStruct((INV_ROWS, BLOCK), jnp.int32),
+            jax.ShapeDtypeStruct((CH, CH), BF16),
         ),
         in_specs=[pl.BlockSpec(memory_space=pltpu.SMEM)] + [vmem] * 3,
-        out_specs=(vmem, vmem),
+        out_specs=(vmem, vmem, vmem),
         scratch_shapes=[
             pltpu.VMEM((GR // 8, 2, 8, 128), F32),
             pltpu.VMEM((NPR * NPC, QR, 128), F32),
             pltpu.VMEM((NPR * NPC, QR, 128), F32),
             pltpu.VMEM((NPR, 1, GR), jnp.int32),
-            pltpu.VMEM((CH, CH), BF16),
             pltpu.VMEM((CH, CH), BF16),
             dma((NPR * NPC,)),
             dma((NPR * NPC,)),
@@ -299,7 +296,7 @@
 
 
 def panel_kernel(
-    inverse, weight_a, weight_b, kaula, rows_hbm, goce_hbm, out,
+    inverse, weight_a, weight_b, kaula, pick, rows_hbm, goce_hbm, out,
     source, goce, raw, a, panel, heads, work, factor_t, w_high, w_low, diag_f, diag_x,
     load, sent0, got0, sent1, got1, sent2, got2, head_sent, head_got,
 ):
@@ -340,10 +337,11 @@
 
         lax.fori_loop(0, size // 16, gather, 0)
         at = slice(start, start + size)
+        arrived = jnp.concatenate([raw[: size // 8, h].reshape(size, BLOCK) for h in range(2)], axis=1)
+        moved = select_columns(arrived, pick[...])
         for h in range(2):
             cols = slice(h * BLOCK, (h + 1) * BLOCK)
-            moved = raw[: size // 8, h].reshape(size, BLOCK)
-            block = weight_a[0] * moved + weight_b[0] * goce[at, cols]
+            block = weight_a[0] * moved[:, cols] + weight_b[0] * goce[at, cols]
             if c == 0:
                 diagonal = iota((BLOCK, BLOCK), 0) == iota((BLOCK, BLOCK), 1)
                 here = (row_id % NPC == col_id) & (row_id // NPC == h)
@@ -483,17 +481,22 @@
 
     next0, next1, next2 = 6, 3, 2
 
-    def advance():
-        nonlocal next0, next1, next2
+    def push():
+        nonlocal next0, next1
         if next0 < NC:
             start0(next0)
         if next1 < NC:
             start1(next1)
+        if next0 + 1 < NC:
+            build(next0 + 1)
+        next0, next1 = next0 + 1, next1 + 1
+
+    def advance():
+        nonlocal next2
         if next2 < NC:
             start2(next2)
-        if next0 + 1 < NC:
-            build(next0 + 1)
-        next0, next1, next2 = next0 + 1, next1 + 1, next2 + 1
+        next2 += 1
+        push()
 
     for copy in fetch:
         copy.wait()
@@ -521,8 +524,11 @@
     advance()
     head_y()
     advance()
+    push()
     head_core()
     advance()
+    push()
+    push()
     head_in()
 
     lower = iota((BLOCK, BLOCK), 0) >= iota((BLOCK, BLOCK), 1)
@@ -629,13 +635,13 @@
     head_done()
 
 
-def panel_step(inverse, weight_a, weight_b, kaula, rows, goce):
+def panel_step(inverse, pick, weight_a, weight_b, kaula, rows, goce):
     dma = pltpu.SemaphoreType.DMA
     smem, anywhere = pl.BlockSpec(memory_space=pltpu.SMEM), pl.BlockSpec(memory_space=pl.ANY)
     return pl.pallas_call(
         panel_kernel,
         out_shape=jax.ShapeDtypeStruct((RH, CH), F32),
-        in_specs=[smem] * 3 + [pl.BlockSpec(memory_space=pltpu.VMEM), anywhere, anywhere],
+        in_specs=[smem] * 3 + [pl.BlockSpec(memory_space=pltpu.VMEM)] * 2 + [anywhere] * 2,
         out_specs=pl.BlockSpec(memory_space=pltpu.VMEM),
         scratch_shapes=[
             pltpu.VMEM((2 * RH, 128), F32),
@@ -664,7 +670,7 @@
             collective_id=0, has_side_effects=True, vmem_limit_bytes=VMEM_LIMIT
         ),
         name="panel_step",
-    )(inverse, weight_a, weight_b, kaula.reshape(1, CH), rows, goce)
+    )(inverse, weight_a, weight_b, kaula.reshape(1, CH), pick, rows, goce)
 
 
 def shards(grace_slab, goce_slab, grace_weight, goce_weight, kaula_prior, row_target, column_target):
@@ -673,8 +679,9 @@
     targets, order = lax.sort((targets, jnp.arange(RH, dtype=jnp.int32)), num_keys=1)
     places = targets.reshape(NPR, 1, GR) - jnp.arange(NPR, dtype=jnp.int32)[:, None, None] * RH
     split_rows = grace_slab.reshape(RH // 8, 8, 2, 128).transpose(0, 2, 1, 3).reshape(2 * RH, 128)
-    rows, inverse = exchange(linear(order), column_target, places, split_rows)
-    return panel_step(inverse, grace_weight, goce_weight, kaula_prior, rows.reshape(2 * RH, 128), goce_slab)
+    rows, inverse, pick = exchange(linear(order), column_target, places, split_rows)
+    rows = rows.reshape(2 * RH, 128)
+    return panel_step(inverse, pick, grace_weight, goce_weight, kaula_prior, rows, goce_slab)
 
 
 def solution(mesh):

time: 244 us -> 238 us (0.975)
  Pallas kernels: 226 us -> 220 us
    pallas_call x1, Pallas kernels: 130 us -> 126 us  [panel_step(): pl.pallas_call(panel_kernel, out_shape=jax.ShapeDtypeStruct((RH, CH), F32...]
    pallas_call x1, Pallas kernels: 95.9 us -> 93.4 us  [exchange(): pl.pallas_call(exchange_kernel, out_shape=(jax.ShapeDtypeStruct((NPR, GR...]
where the time goes in v5:
time: 238 us; the launch traced here: 235 us
  Pallas kernels  220 us (92%)
  other arithmetic  7.48 us (3%)
  local copies, waits for them, and re-layouts  6.47 us (3%)
    pallas_call x1, Pallas kernels, panel_step(): pl.pallas_call(panel_kernel, out_shape=jax.ShapeDtypeStruct((RH, CH), F32...  126 us
    pallas_call x1, Pallas kernels, exchange(): pl.pallas_call(exchange_kernel, out_shape=(jax.ShapeDtypeStruct((NPR, GR...  93.4 us
    sort x1, other arithmetic, shards(): lax.sort((targets, jnp.arange(RH, dtype=jnp.int32)), num_keys=1)  6.16 us
    unnamed x1, local copies, waits for them, and re-layouts  5.54 us

profile of v5, /device:TPU:7, one launch (start us, length us, event | category | flops | bytes accessed | tf_op | source)
XLA Modules:
  0.0 234.8 jit_solution(8645249161093437595)
XLA Ops:
  1.3 0.8 dynamic_slice.3
  2.1 6.2 %sort.15 = (s32[5632]{0:T(1024)S(1)}, s32[5632]{0:T(1024)S(1)}) sort(s32[5632]{0:T(1024)S(1)} %dynamic_slice.3, s32[5632]{0:T(1024)S(1)} %iota.8), dimensions={0}, to_apply=%region_0.0 | sort | flops 73216 | bytes 90112 | tf_op jit(solution)/shard_map/sort | solution.py:679
  8.3 0.6 fusion.1.order
  8.9 0.1 reshape.57
  9.0 0.7 broadcast_subtract_fusion.places
  9.7 93.4 %exchange.1 = (f32[16,44,2,8,128]{4,3,2,1,0:T(8,128)}, s32[48,128]{1,0:T(8,128)}, bf16[256,256]{1,0:T(8,128)(2,1)}) custom-call(s32[5632]{0:T(1024)} %fusion.1.order, s32[16,128]{1,0:T(8,128)} %bitcast.10, s32[16,1,352]{2,1,0:T(1,128)} %broadcast_subtract_fusion.places, f32[11264,128]{1,0:T(8,128)} %bitcast.9), custom_call_target="tpu_custom_call" | custom-call | tf_op jit(solution)/shard_map/exchange/pallas_call | solution.py:225
  103.1 126.2 %panel_step.1 = f32[5632,256]{1,0:T(8,128)} custom-call(s32[48,128]{1,0:T(8,128)} %get-tuple-element.12.inverse, f32[1]{0:T(128)S(6)} %copy.9.weight_a, f32[1]{0:T(128)S(6)} %copy.10.weight_b, f32[1,256]{1,0:T(1,128)} %bitcast.11, bf16[256,256]{1,0:T(8,128)(2,1)} %get-tuple-element.13.pick, f32[11264,128]{1,0:T(8,128)} %bitcast.8, f32[5632,256]{1,0:T(8,128)} %goce_hbm.1), custom_call_target="tpu_custom_call" | custom-call | tf_op jit(solution)/shard_map/panel_step/pallas_call | solution.py:641
  229.3 5.5 %copy.11 = f32[5632,256]{1,0:T(8,128)} copy(f32[5632,256]{1,0:T(8,128)} %panel_step.1) | data formatting | bytes 11534336
  (2 shorter events, 0.0 us)

commit v6 on v5

--- a/solution.py
+++ b/solution.py
@@ -17,7 +17,7 @@
 QR = GR // 4
 PIECES = [(0, BLOCK)] + [(at, 256) for at in range(BLOCK, RH - 256, 256)] + [(RH - BLOCK, BLOCK)]
 NC = len(PIECES)
-VMEM_LIMIT = 60 * 2**20
+VMEM_LIMIT = 62 * 2**20
 INV_ROWS = 48
 
 
@@ -57,7 +57,7 @@
     return jnp.bitwise_xor(col_id, lax.rem(k + row_id, NPC))
 
 
-def exchange_kernel(
+def exchange_part(
     order, col_all, places, x, out, inverse_out, pick_in,
     rows, packed, received, places_in, pick_out, sent, got, place_sent, place_got,
 ):
@@ -194,7 +194,7 @@
         return total
 
     number = lax.fori_loop(0, NPR, invert, jnp.zeros((INV_ROWS, BLOCK), F32)).astype(jnp.int32)
-    inverse_out[...] = number + lax.shift_right_logical(number, 3) * 8
+    inverse_out[...] = jnp.minimum(jnp.maximum(number, 0), RH - 1)
 
     def arrive(step, carry):
         origin = turn_row(row_id, col_id, step)
@@ -202,51 +202,25 @@
         halves = [regroup([received[origin * NPC + h * 4 + q] for q in range(4)], lane) for h in range(2)]
         joined = [jnp.concatenate(half, axis=0) for half in halves]
         for h in range(2):
-            out[origin, :, h] = joined[h].reshape(GR // 8, 8, 128)
+            out[pl.ds(origin * (GR // 8), GR // 8), h] = joined[h].reshape(GR // 8, 8, 128)
         return carry
 
     lax.fori_loop(0, NPR, arrive, 0)
 
-    def leave(step, carry):
-        each(step, lambda r, c: chunk_copy(r, c).wait_send(), None)
-        return carry
-
-    lax.fori_loop(0, NPR, leave, 0)
-
-    def announced(k, carry):
-        place_copy(jnp.bitwise_xor(row_id, k), row_id).wait_send()
-        return carry
-
-    lax.fori_loop(1, NPR, announced, 0)
-
-
-def exchange(order, col_all, places, x):
-    dma, vmem = pltpu.SemaphoreType.DMA, pl.BlockSpec(memory_space=pltpu.VMEM)
-    return pl.pallas_call(
-        exchange_kernel,
-        out_shape=(
-            jax.ShapeDtypeStruct((NPR, GR // 8, 2, 8, 128), F32),
-            jax.ShapeDtypeStruct((INV_ROWS, BLOCK), jnp.int32),
-            jax.ShapeDtypeStruct((CH, CH), BF16),
-        ),
-        in_specs=[pl.BlockSpec(memory_space=pltpu.SMEM)] + [vmem] * 3,
-        out_specs=(vmem, vmem, vmem),
-        scratch_shapes=[
-            pltpu.VMEM((GR // 8, 2, 8, 128), F32),
-            pltpu.VMEM((NPR * NPC, QR, 128), F32),
-            pltpu.VMEM((NPR * NPC, QR, 128), F32),
-            pltpu.VMEM((NPR, 1, GR), jnp.int32),
-            pltpu.VMEM((CH, CH), BF16),
-            dma((NPR * NPC,)),
-            dma((NPR * NPC,)),
-            dma((NPR,)),
-            dma((NPR,)),
-        ],
-        compiler_params=pltpu.CompilerParams(
-            collective_id=1, has_side_effects=True, vmem_limit_bytes=VMEM_LIMIT
-        ),
-        name="exchange",
-    )(order, col_all.reshape(16, 128), places, x)
+    def finish():
+        def leave(step, carry):
+            each(step, lambda r, c: chunk_copy(r, c).wait_send(), None)
+            return carry
+
+        lax.fori_loop(0, NPR, leave, 0)
+
+        def announced(k, carry):
+            place_copy(jnp.bitwise_xor(row_id, k), row_id).wait_send()
+            return carry
+
+        lax.fori_loop(1, NPR, announced, 0)
+
+    return finish
 
 
 def across_rows(v, s):
@@ -295,9 +269,10 @@
     return tuple([pltpu.roll(v, 120, 1) for v in d[1:] + d[:1]] + x[1:] + x[:1])
 
 
-def panel_kernel(
-    inverse, weight_a, weight_b, kaula, pick, rows_hbm, goce_hbm, out,
-    source, goce, raw, a, panel, heads, work, factor_t, w_high, w_low, diag_f, diag_x,
+def step_kernel(
+    order, weight_a, weight_b, kaula, col_all, places, x, goce_hbm, out,
+    rows, packed, received, places_in, pick_out, sent, got, place_sent, place_got,
+    inverse_vector, inverse, pick, source, goce, raw, a, panel, heads, work, factor_t, w_high, w_low, diag_f, diag_x,
     load, sent0, got0, sent1, got1, sent2, got2, head_sent, head_got,
 ):
     row_id, col_id = lax.axis_index("prow"), lax.axis_index("pcol")
@@ -314,15 +289,14 @@
     y_near = (cz * 4 + lax.rem(cyc + 2, 4), col_id)
     core_mate = (cz * 4 + cyc + 1 - 2 * core, col_id)
 
-    fetch = [
-        pltpu.make_async_copy(rows_hbm, source, load.at[0]),
-        pltpu.make_async_copy(goce_hbm, goce, load.at[1]),
-    ]
-    for copy in fetch:
-        copy.start()
-    barrier = pltpu.get_barrier_semaphore()
-    for device in [cross, x_mate, y_mate, y_near, core_mate] + over_z:
-        pl.semaphore_signal(barrier, inc=1, device_id=device, device_id_type=MESH)
+    fetch = pltpu.make_async_copy(goce_hbm, goce, load.at[1])
+    fetch.start()
+    finish_exchange = exchange_part(
+        order, col_all, places, x, source, inverse_vector, pick,
+        rows, packed, received, places_in, pick_out, sent, got, place_sent, place_got,
+    )
+    to_scalars = pltpu.make_async_copy(inverse_vector, inverse, load.at[0])
+    to_scalars.start()
 
     def build(c):
         start, size = PIECES[c]
@@ -331,8 +305,9 @@
             for u in range(16):
                 at = inverse[start // 128 + i // 8, i % 8 * 16 + u]
                 tile, sub = i * 2 + u // 8, u % 8
-                raw[tile, 0, sub : sub + 1, :] = source[pl.ds(at, 1), :]
-                raw[tile, 1, sub : sub + 1, :] = source[pl.ds(at + 8, 1), :]
+                origin, row = lax.shift_right_logical(at, 3), jnp.bitwise_and(at, 7)
+                raw[tile, 0, sub : sub + 1, :] = source[origin, 0, pl.ds(row, 1), :]
+                raw[tile, 1, sub : sub + 1, :] = source[origin, 1, pl.ds(row, 1), :]
             return carry
 
         lax.fori_loop(0, size // 16, gather, 0)
@@ -498,10 +473,9 @@
         next2 += 1
         push()
 
-    for copy in fetch:
-        copy.wait()
+    to_scalars.wait()
+    fetch.wait()
     build(0)
-    pl.semaphore_wait(barrier, 8)
     build(1)
     start0(0)
     build(2)
@@ -633,18 +607,31 @@
         send(own, c, sent2.at[c, 0], got2.at[c, 0], mate2).wait_send()
         send(j1, c, sent2.at[c, 1], got2.at[c, 1], mate2).wait_send()
     head_done()
-
-
-def panel_step(inverse, pick, weight_a, weight_b, kaula, rows, goce):
-    dma = pltpu.SemaphoreType.DMA
+    finish_exchange()
+
+
+def step(order, weight_a, weight_b, kaula, col_all, places, x, goce):
+    dma, vmem = pltpu.SemaphoreType.DMA, pl.BlockSpec(memory_space=pltpu.VMEM)
     smem, anywhere = pl.BlockSpec(memory_space=pltpu.SMEM), pl.BlockSpec(memory_space=pl.ANY)
     return pl.pallas_call(
-        panel_kernel,
+        step_kernel,
         out_shape=jax.ShapeDtypeStruct((RH, CH), F32),
-        in_specs=[smem] * 3 + [pl.BlockSpec(memory_space=pltpu.VMEM)] * 2 + [anywhere] * 2,
+        in_specs=[smem] * 3 + [vmem] * 4 + [anywhere],
         out_specs=pl.BlockSpec(memory_space=pltpu.VMEM),
         scratch_shapes=[
-            pltpu.VMEM((2 * RH, 128), F32),
+            pltpu.VMEM((GR // 8, 2, 8, 128), F32),
+            pltpu.VMEM((NPR * NPC, QR, 128), F32),
+            pltpu.VMEM((NPR * NPC, QR, 128), F32),
+            pltpu.VMEM((NPR, 1, GR), jnp.int32),
+            pltpu.VMEM((CH, CH), BF16),
+            dma((NPR * NPC,)),
+            dma((NPR * NPC,)),
+            dma((NPR,)),
+            dma((NPR,)),
+            pltpu.VMEM((INV_ROWS, BLOCK), jnp.int32),
+            pltpu.SMEM((INV_ROWS, BLOCK), jnp.int32),
+            pltpu.VMEM((CH, CH), BF16),
+            pltpu.VMEM((RH // 8, 2, 8, 128), F32),
             pltpu.VMEM((RH, CH), F32),
             pltpu.VMEM((32, 2, 8, 128), F32),
             pltpu.VMEM((2, RH, BLOCK), F32),
@@ -669,8 +656,8 @@
         compiler_params=pltpu.CompilerParams(
             collective_id=0, has_side_effects=True, vmem_limit_bytes=VMEM_LIMIT
         ),
-        name="panel_step",
-    )(inverse, weight_a, weight_b, kaula.reshape(1, CH), pick, rows, goce)
+        name="step",
+    )(order, weight_a, weight_b, kaula.reshape(1, CH), col_all.reshape(16, 128), places, x, goce)
 
 
 def shards(grace_slab, goce_slab, grace_weight, goce_weight, kaula_prior, row_target, column_target):
@@ -679,9 +666,9 @@
     targets, order = lax.sort((targets, jnp.arange(RH, dtype=jnp.int32)), num_keys=1)
     places = targets.reshape(NPR, 1, GR) - jnp.arange(NPR, dtype=jnp.int32)[:, None, None] * RH
     split_rows = grace_slab.reshape(RH // 8, 8, 2, 128).transpose(0, 2, 1, 3).reshape(2 * RH, 128)
-    rows, inverse, pick = exchange(linear(order), column_target, places, split_rows)
-    rows = rows.reshape(2 * RH, 128)
-    return panel_step(inverse, pick, grace_weight, goce_weight, kaula_prior, rows, goce_slab)
+    return step(
+        linear(order), grace_weight, goce_weight, kaula_prior, column_target, places, split_rows, goce_slab
+    )
 
 
 def solution(mesh):

time: 238 us -> 234 us (0.983)
  Pallas kernels: 220 us -> 215 us
    pallas_call x2 -> x1, Pallas kernels: 220 us -> 215 us  [step(): pl.pallas_call(step_kernel, out_shape=jax.ShapeDtypeStruct((RH, CH), F32)...]
where the time goes in v6:
time: 234 us; the launch traced here: 231 us
  Pallas kernels  215 us (92%)
  other arithmetic  7.48 us (3%)
  local copies, waits for them, and re-layouts  6.47 us (3%)
    pallas_call x1, Pallas kernels, step(): pl.pallas_call(step_kernel, out_shape=jax.ShapeDtypeStruct((RH, CH), F32)...  215 us
    sort x1, other arithmetic, shards(): lax.sort((targets, jnp.arange(RH, dtype=jnp.int32)), num_keys=1)  6.16 us
    unnamed x1, local copies, waits for them, and re-layouts  5.54 us

profile of v6, /device:TPU:7, one launch (start us, length us, event | category | flops | bytes accessed | tf_op | source)
XLA Modules:
  0.0 230.6 jit_solution(14135629011378973197)
XLA Ops:
  1.3 0.8 dynamic_slice.3
  2.1 6.2 %sort.15 = (s32[5632]{0:T(1024)S(1)}, s32[5632]{0:T(1024)S(1)}) sort(s32[5632]{0:T(1024)S(1)} %dynamic_slice.3, s32[5632]{0:T(1024)S(1)} %iota.8), dimensions={0}, to_apply=%region_0.0 | sort | flops 73216 | bytes 90112 | tf_op jit(solution)/shard_map/sort | solution.py:666
  8.3 0.6 fusion.1.order
  8.9 0.1 reshape.55
  9.0 0.7 broadcast_subtract_fusion.places
  9.7 215.3 %step.1 = f32[5632,256]{1,0:T(8,128)} custom-call(s32[5632]{0:T(1024)} %fusion.1.order, f32[1]{0:T(128)S(6)} %copy.9.weight_a, f32[1]{0:T(128)S(6)} %copy.10.weight_b, f32[1,256]{1,0:T(1,128)} %bitcast.9, s32[16,128]{1,0:T(8,128)} %bitcast.8, s32[16,1,352]{2,1,0:T(1,128)} %broadcast_subtract_fusion.places, f32[11264,128]{1,0:T(8,128)} %bitcast.7, ...), custom_call_target="tpu_custom_call" | custom-call | tf_op jit(solution)/shard_map/step/pallas_call | solution.py:616
  225.0 5.5 %copy.11 = f32[5632,256]{1,0:T(8,128)} copy(f32[5632,256]{1,0:T(8,128)} %step.1) | data formatting | bytes 11534336
  (2 shorter events, 0.0 us)

commit v7 on v6

--- a/solution.py
+++ b/solution.py
@@ -270,9 +270,9 @@
 
 
 def step_kernel(
-    order, weight_a, weight_b, kaula, col_all, places, x, goce_hbm, out,
+    order, weight_a, weight_b, kaula, col_all, places, x, goce_hbm, out_hbm,
     rows, packed, received, places_in, pick_out, sent, got, place_sent, place_got,
-    inverse_vector, inverse, pick, source, goce, raw, a, panel, heads, work, factor_t, w_high, w_low, diag_f, diag_x,
+    out, written, inverse_vector, inverse, pick, source, goce, raw, a, panel, heads, work, factor_t, w_high, w_low, diag_f, diag_x,
     load, sent0, got0, sent1, got1, sent2, got2, head_sent, head_got,
 ):
     row_id, col_id = lax.axis_index("prow"), lax.axis_index("pcol")
@@ -585,16 +585,24 @@
                 out[:BLOCK, :BLOCK] = jnp.where(own_panel, jnp.transpose(block), a[0, :BLOCK])
                 out[:BLOCK, BLOCK:] = a[1, :BLOCK]
 
+    def write(c):
+        at = pl.ds(*PIECES[c])
+        return pltpu.make_async_copy(out.at[at], out_hbm.at[at], written.at[c])
+
     done = 0
     while next2 < NC:
         advance()
         for _ in range(2):
             if done <= next2 - 4:
                 update(done)
+                if done:
+                    write(done - 1).start()
                 done += 1
     while done < NC:
         update(done)
+        write(done - 1).start()
         done += 1
+    write(NC - 1).start()
 
     for c in range(NC):
 
@@ -608,6 +616,8 @@
         send(j1, c, sent2.at[c, 1], got2.at[c, 1], mate2).wait_send()
     head_done()
     finish_exchange()
+    for c in range(NC):
+        write(c).wait()
 
 
 def step(order, weight_a, weight_b, kaula, col_all, places, x, goce):
@@ -617,7 +627,7 @@
         step_kernel,
         out_shape=jax.ShapeDtypeStruct((RH, CH), F32),
         in_specs=[smem] * 3 + [vmem] * 4 + [anywhere],
-        out_specs=pl.BlockSpec(memory_space=pltpu.VMEM),
+        out_specs=anywhere,
         scratch_shapes=[
             pltpu.VMEM((GR // 8, 2, 8, 128), F32),
             pltpu.VMEM((NPR * NPC, QR, 128), F32),
@@ -628,6 +638,8 @@
             dma((NPR * NPC,)),
             dma((NPR,)),
             dma((NPR,)),
+            pltpu.VMEM((RH, CH), F32),
+            dma((NC,)),
             pltpu.VMEM((INV_ROWS, BLOCK), jnp.int32),
             pltpu.SMEM((INV_ROWS, BLOCK), jnp.int32),
             pltpu.VMEM((CH, CH), BF16),

time: 234 us -> 232 us (level)
    pallas_call x1, Pallas kernels: 215 us -> 213 us  [step(): pl.pallas_call(step_kernel, out_shape=jax.ShapeDtypeStruct((RH, CH), F32)...]
where the time goes in v7:
time: 232 us; the launch traced here: 228 us
  Pallas kernels  213 us (92%)
  other arithmetic  7.48 us (3%)
  local copies, waits for them, and re-layouts  6.47 us (3%)
    pallas_call x1, Pallas kernels, step(): pl.pallas_call(step_kernel, out_shape=jax.ShapeDtypeStruct((RH, CH), F32)...  213 us
    sort x1, other arithmetic, shards(): lax.sort((targets, jnp.arange(RH, dtype=jnp.int32)), num_keys=1)  6.16 us
    unnamed x1, local copies, waits for them, and re-layouts  5.54 us

profile of v7, /device:TPU:7, one launch (start us, length us, event | category | flops | bytes accessed | tf_op | source)
XLA Modules:
  0.0 228.2 jit_solution(6555128753680575365)
XLA Ops:
  1.3 0.8 dynamic_slice.3
  2.1 6.2 %sort.15 = (s32[5632]{0:T(1024)S(1)}, s32[5632]{0:T(1024)S(1)}) sort(s32[5632]{0:T(1024)S(1)} %dynamic_slice.3, s32[5632]{0:T(1024)S(1)} %iota.8), dimensions={0}, to_apply=%region_0.0 | sort | flops 73216 | bytes 90112 | tf_op jit(solution)/shard_map/sort | solution.py:678
  8.3 0.6 fusion.1.order
  8.9 0.1 reshape.55
  9.0 0.7 broadcast_subtract_fusion.places
  9.7 212.9 %step.1 = f32[5632,256]{1,0:T(8,128)} custom-call(s32[5632]{0:T(1024)} %fusion.1.order, f32[1]{0:T(128)S(6)} %copy.9.weight_a, f32[1]{0:T(128)S(6)} %copy.10.weight_b, f32[1,256]{1,0:T(1,128)} %bitcast.9, s32[16,128]{1,0:T(8,128)} %bitcast.8, s32[16,1,352]{2,1,0:T(1,128)} %broadcast_subtract_fusion.places, f32[11264,128]{1,0:T(8,128)} %bitcast.7, ...), custom_call_target="tpu_custom_call" | custom-call | tf_op jit(solution)/shard_map/step/pallas_call | solution.py:626
  222.7 5.5 %copy.11 = f32[5632,256]{1,0:T(8,128)} copy(f32[5632,256]{1,0:T(8,128)} %step.1) | data formatting | bytes 11534336
  (2 shorter events, 0.0 us)
